TPU v7x, 32 devices: a whole 2x2x4 slice. The times are simulated.
32 devices in a mesh: groups: 2 (over y), pcol: 8 (over z, x), prow: 2 (over core).
Axes of the slice: x: 2, y: 2, z: 4, core: 2. Of those that a mesh axis runs over, the one named last changes fastest.
Arguments:
- leaf_inverse: bfloat16 [512, 128, 128], P(('groups', 'pcol', 'prow')), parts along dimension 0, as said below
- leaf_rhs: bfloat16 [65536, 256], P(('groups', 'pcol', 'prow')), parts along dimension 0, may hold values from -6 to 6
- leaf_coupling: bfloat16 [128, 65536], P(None, ('groups', 'pcol', 'prow')), parts along dimension 1, may hold values from -0.125 to 0.125
- parent: int32 [512], P(('groups', 'pcol', 'prow')), parts along dimension 0, may hold values from 0 to 1
- sep_inverse: float32 [16, 128, 128], P(('groups', 'pcol')), parts along dimension 0, as said below
- sep_coupling: float32 [16, 128, 128], P(('groups', 'pcol')), parts along dimension 0, may hold values from -0.375 to 0.375
- sep_rhs: float32 [2048, 256], P(('groups', 'pcol'), 'prow'), parts along dimension 0, may hold values from -6 to 6
Outputs:
- leaf_solution: bfloat16 [65536, 256], P(('groups', 'pcol', 'prow')), parts along dimension 0
- sep_solution: float32 [2048, 256], P(('groups', 'pcol'), 'prow'), parts along dimension 0
There are 2 independent parts, one for each index of `groups`. A program takes and returns all parts, laid end to end along the dimension named above; each array names one. Nothing has to cross between parts.
Inputs may be any that keep to these rules, and one draw needn't show every extreme that they name: `leaf_inverse`: each block is lower triangular with a positive diagonal. `sep_inverse`: each block is lower triangular with a positive diagonal.
All inputs are finite; a program needn't handle non-finite values.
Results may differ from a plain program's by a relative error of at most 0.0026.
Values sent between devices are 32-bit elements; how exact they have to be, the bound alone decides.
No kernel may reach another device: no remote copies, remote signals or barrier semaphores. Data moves between devices by JAX's collectives and lax.ppermute only.
A program may use at most 128 MiB of HBM per device.

v0:
```python
import jax
import jax.numpy as jnp
from jax import lax
from jax.sharding import PartitionSpec as P


def shifted(array, axis, by):
    peers = lax.axis_size(axis)
    pairs = [(i, i + by) for i in range(peers) if 0 <= i + by < peers]
    return lax.ppermute(array, axis, pairs)


def entering(part, axis, combine, identity):
    place = lax.axis_index(axis)
    gathered = jax.tree.map(lambda a: lax.all_gather(a, axis), part)
    state = jax.tree.map(lambda a, e: jnp.zeros_like(a) + jnp.asarray(e, a.dtype), part, identity)

    def one(lap, state):
        return combine(
            state, jax.tree.map(lambda a: lax.dynamic_index_in_dim(a, lap, 0, False), gathered)
        )

    return lax.fori_loop(0, place, one, state)


def on_device(leaf_inverse, leaf_rhs, leaf_coupling, parent, sep_inverse, sep_coupling, sep_rhs):
    count = leaf_inverse.shape[0]
    block = leaf_inverse.shape[1]
    width = leaf_rhs.shape[1]
    blocks = leaf_rhs.reshape(count, block, width)
    solved = jnp.einsum(
        "jab,jbr->jar", leaf_inverse, blocks, preferred_element_type=jnp.float32
    ).astype(jnp.bfloat16)
    own_mask = (parent == 0).astype(jnp.bfloat16)[:, None, None]
    next_mask = (parent == 1).astype(jnp.bfloat16)[:, None, None]
    own_part = jnp.dot(
        leaf_coupling,
        (solved * own_mask).reshape(count * block, width),
        preferred_element_type=jnp.float32,
    )
    next_part = jnp.dot(
        leaf_coupling,
        (solved * next_mask).reshape(count * block, width),
        preferred_element_type=jnp.float32,
    )
    arrived = shifted(next_part, "pcol", 1)
    update = lax.psum_scatter(own_part + arrived, "prow", scatter_dimension=1, tiled=True)
    highest = lax.Precision.HIGHEST
    inverse = sep_inverse[0]
    coupling = sep_coupling[0]
    first = lax.axis_index("pcol") == 0
    step_map = -jnp.dot(inverse, coupling, precision=highest)
    step_map = jnp.where(first, jnp.zeros_like(step_map), step_map)
    offset = jnp.dot(inverse, sep_rhs - update, precision=highest)

    def compose(earlier, later):
        return (
            jnp.dot(later[0], earlier[0], precision=highest),
            jnp.dot(later[0], earlier[1], precision=highest) + later[1],
        )

    identity = (jnp.eye(block, dtype=jnp.float32), jnp.zeros_like(offset))
    prior = entering((step_map, offset), "pcol", compose, identity)
    solution = jnp.dot(step_map, prior[1], precision=highest) + offset
    return (solved.reshape(count * block, width), solution)


def solution(mesh):
    return jax.shard_map(
        on_device,
        mesh=mesh,
        in_specs=(
            P(("groups", "pcol", "prow"), None, None),
            P(("groups", "pcol", "prow"), None),
            P(None, ("groups", "pcol", "prow")),
            P(("groups", "pcol", "prow")),
            P(("groups", "pcol"), None, None),
            P(("groups", "pcol"), None, None),
            P(("groups", "pcol"), "prow"),
        ),
        out_specs=(P(("groups", "pcol", "prow"), None), P(("groups", "pcol"), "prow")),
        check_vma=False,
    )
```

profile of v0, /device:TPU:0, one launch (start us, length us, event | category | flops | bytes accessed | tf_op | source)
XLA Modules:
  0.0 94.5 jit_solution(13562522655162906647)
XLA Ops:
  7.2 0.0 copy-start
  7.2 0.0 reduce-scatter.2.cloned.1.call-start
  7.2 0.7 compare_convert_fusion.1
  8.0 0.4 copy-done
  8.4 0.0 copy-start.1
  8.4 2.5 %broadcast_multiply_fusion.1 = (bf16[16,128,256]{2,1,0:T(8,128)(2,1)S(1)}, bf16[16,128,256]{2,1,0:T(8,128)(2,1)S(1)}, bf16[16,128,256]{2,1,0:T(8,128)(2,1)}) fusion(bf16[16]{0:T(256)(128)(2,1)S(1)} %get-tuple-element.66, bf16[16]{0:T(256)(128)(2,1)S(1)} %get-tuple-element.67, bf16[16,128,128]{2,1,0:T(8,128)(2,1)} %param.9, ...), kind=kOutput, calls=%fused_computation.13 | convolution fusion | flops 135790592 | bytes 4718656 | tf_op jit(solution)/shard_map/jab,jbr->jar/dot_general | solution.py:31
  10.9 0.0 copy-done.1
  10.9 0.3 convolution_bitcast_fusion
  11.2 0.0 copy-start.2
  11.2 0.0 copy-start.3
  11.3 5.0 %collective-permute-start = (f32[128,256]{1,0:T(8,128)S(1)}, f32[128,256]{1,0:T(8,128)S(1)}, u32[]{:S(2)}, u32[]{:S(2)}) collective-permute-start(f32[128,256]{1,0:T(8,128)S(1)} %convolution_bitcast_fusion), channel_id=1, source_target_pairs={{0,2},{2,4},{4,6},{6,8},{8,10},{10,12},{12,14},{1,3},{3,5},{5,7},{... | collective-permute-start | bytes 393224 | tf_op jit(solution)/shard_map/ppermute | solution.py:10
  16.3 2.7 %collective-permute-done = f32[128,256]{1,0:T(8,128)S(1)} collective-permute-done((f32[128,256]{1,0:T(8,128)S(1)}, f32[128,256]{1,0:T(8,128)S(1)}, u32[]{:S(2)}, u32[]{:S(2)}) %collective-permute-start) | collective-permute-done | bytes 131104 | tf_op jit(solution)/shard_map/ppermute | solution.py:10
  19.0 0.0 copy-start.4
  19.0 1.0 %fusion.3 = f32[128,256]{1,0:T(8,128)} fusion(f32[128,256]{1,0:T(8,128)S(1)} %collective-permute-done, bf16[128,2048]{1,0:T(8,128)(2,1)S(1)} %copy-done.1, bf16[2048,256]{1,0:T(8,128)(2,1)S(1)} %bitcast.43), kind=kOutput, calls=%fused_computation.7 | convolution fusion | flops 134250496 | bytes 1835008 | tf_op jit(solution)/shard_map/dot_general | solution.py:36
  19.9 0.0 reduce-scatter.2.cloned.1.call-update
  20.0 0.0 copy-done.2
  20.0 0.0 copy-done.3
  20.0 0.2 fusion.4
  20.2 33.6 %all-gather = f32[1024,128]{1,0:T(8,128)S(1)} all-gather(f32[128,128]{1,0:T(8,128)S(1)} %fusion.4), channel_id=2, replica_groups=mesh['groups'=2,'pcol'=8,'prow'=2] {'pcol'}, dimensions={0}, use_global_device_ids=true | all-gather | bytes 589824 | tf_op jit(solution)/shard_map/all_gather | solution.py:15
  53.8 0.0 reduce-scatter.2.cloned.1.call-done
  53.8 0.0 copy-done.4
  53.8 1.1 %convolution_bitcast_fusion.2 = f32[128,128]{0,1:T(8,128)S(1)} fusion(f32[1,128,128]{2,1,0:T(8,128)S(1)} %copy-done.2, f32[128,128]{1,0:T(8,128)S(1)} %copy-done.4, f32[128,128]{1,0:T(8,128)} %reduce-scatter.2.cloned.1.call-done), kind=kOutput, calls=%fused_computation.9 | convolution fusion | flops 25182208 | bytes 262144 | tf_op jit(solution)/shard_map/dot_general | solution.py:54
  55.0 31.5 %all-gather.1 = f32[1024,128]{0,1:T(8,128)S(1)} all-gather(f32[128,128]{0,1:T(8,128)S(1)} %convolution_bitcast_fusion.2), channel_id=3, replica_groups=mesh['groups'=2,'pcol'=8,'prow'=2] {'pcol'}, dimensions={0}, use_global_device_ids=true | all-gather | bytes 589824 | tf_op jit(solution)/shard_map/all_gather | solution.py:15
  86.4 0.2 copy.13
  86.6 0.3 convolution_add_fusion.1
  86.9 0.7 copy.11
  (2 shorter events, 0.0 us)
Async XLA Ops:
  7.2 1.2 %copy-start = (bf16[2048,256]{1,0:T(8,128)(2,1)S(1)}, bf16[2048,256]{1,0:T(8,128)(2,1)}, u32[]{:S(2)}) copy-start(bf16[2048,256]{1,0:T(8,128)(2,1)} %param.10) | copy-start | bytes 3145732
  7.2 46.6 %reduce-scatter.2.cloned.1.call-start = ((), (), s32[]{:S(2)}) async-start(), calls=%async_computation.1 | async-start | bytes 196608 | tf_op jit(solution)/shard_map/reduce_scatter | solution.py:47
  8.4 2.5 %copy-start.1 = (bf16[128,2048]{1,0:T(8,128)(2,1)S(1)}, bf16[128,2048]{1,0:T(8,128)(2,1)}, u32[]{:S(2)}) copy-start(bf16[128,2048]{1,0:T(8,128)(2,1)} %param.11) | copy-start | bytes 1572868
  11.2 8.7 %copy-start.2 = (f32[1,128,128]{2,1,0:T(8,128)S(1)}, f32[1,128,128]{2,1,0:T(8,128)}, u32[]{:S(2)}) copy-start(f32[1,128,128]{2,1,0:T(8,128)} %param.13) | copy-start | bytes 196612
  11.2 8.7 %copy-start.3 = (f32[1,128,128]{2,1,0:T(8,128)S(1)}, f32[1,128,128]{2,1,0:T(8,128)}, u32[]{:S(2)}) copy-start(f32[1,128,128]{2,1,0:T(8,128)} %param.14) | copy-start | bytes 196612
  11.3 7.7 %collective-permute-start = (f32[128,256]{1,0:T(8,128)S(1)}, f32[128,256]{1,0:T(8,128)S(1)}, u32[]{:S(2)}, u32[]{:S(2)}) collective-permute-start(f32[128,256]{1,0:T(8,128)S(1)} %convolution_bitcast_fusion), channel_id=1, source_target_pairs={{0,2},{2,4},{4,6},{6,8},{8,10},{10,12},{12,14},{1,3},{3,5},{5,7},{... | collective-permute-start | bytes 393224 | tf_op jit(solution)/shard_map/ppermute | solution.py:10
  19.0 34.9 %copy-start.4 = (f32[128,128]{1,0:T(8,128)S(1)}, f32[128,128]{1,0:T(8,128)}, u32[]{:S(2)}) copy-start(f32[128,128]{1,0:T(8,128)} %param.15) | copy-start | bytes 196612
Sparse Core Ops, SparseCore 0:
  20.1 9.7 reduce-scatter.1
where the time goes:
time: 94.8 us; the launch traced here: 94.5 us
  blocking collectives  65.1 us (69%)
  between operations  14.1 us (15%)
  matrix products  5.38 us (6%)
  starting transfers between devices  5.03 us (5%)
  waiting for transfers between devices  2.73 us (3%)
  local copies, waits for them, and re-layouts  1.4 us (1%)
    all_gather x2, blocking collectives, entering(): gathered = jax.tree.map(lambda a: lax.all_gather(a, axis), part)  65.1 us
    ppermute x1, starting transfers between devices, shifted(): return lax.ppermute(array, axis, pairs)  4.99 us
    ppermute x1, waiting for transfers between devices, shifted(): return lax.ppermute(array, axis, pairs)  2.71 us
    dot_general x1, matrix products, on_device(): jnp.einsum('jab,jbr->jar', leaf_inverse, blocks, preferred_element_type=j...  2.49 us
  transfers between devices with their start and end apart: 2, of which 1 were waited for; matrix products, arithmetic and copies ran while one was open for 0% of the time, Pallas kernels for 0%

commit v1 on v0

v1 whole, which is shorter than its diff:
```python
import jax
import jax.numpy as jnp
from jax import lax
from jax.sharding import PartitionSpec as P


def mul(a, b):
    return jnp.dot(a, b, precision=lax.Precision.HIGH)


def on_device(leaf_inverse, leaf_rhs, leaf_coupling, parent, sep_inverse, sep_coupling, sep_rhs):
    count, block = leaf_inverse.shape[:2]
    width = leaf_rhs.shape[1]
    half = width // 2
    columns = lax.axis_size("pcol")
    column = lax.axis_index("pcol")
    inverse = sep_inverse[0]
    ahead = lax.ppermute(sep_coupling[0], "pcol", [(i, (i - 1) % columns) for i in range(columns)])

    solved = jnp.einsum(
        "jab,jbr->jar",
        leaf_inverse,
        leaf_rhs.reshape(count, block, width),
        preferred_element_type=jnp.float32,
    ).astype(jnp.bfloat16)
    solved = solved.reshape(count * block, width)
    link = jnp.repeat(parent, block)[None, :]
    zero = jnp.zeros_like(leaf_coupling)
    both = jnp.concatenate(
        [jnp.where(link == 0, leaf_coupling, zero), jnp.where(link == 1, leaf_coupling, zero)], 0
    )
    sums = jnp.dot(both, solved, preferred_element_type=jnp.float32)
    row = lax.axis_index("prow")
    left, right = sums[:, :half], sums[:, half:]
    kept = jnp.where(row == 0, left, right)
    sent = jnp.where(row == 0, right, left)
    sums = kept + lax.ppermute(sent, "prow", [(0, 1), (1, 0)])
    own, onward = sums[:block], sums[block:]

    found = mul(inverse, sep_rhs - own)
    weight = inverse
    total = mul(ahead, jnp.concatenate([found, -inverse], 1))
    total = jnp.concatenate([total[:, :half] + onward, total[:, half:]], 1)
    distance = 1
    while distance < columns:
        last = 2 * distance >= columns
        pairs = [(i, i ^ distance) for i in range(columns) if i ^ distance < columns]
        came = lax.ppermute(total[:, :half] if last else total, "pcol", pairs)
        upper = (column & distance) != 0
        came_e = came[:, :half]
        found = jnp.where(upper, found - mul(weight, came_e), found)
        if not last:
            came_b = came[:, half:]
            weight = jnp.where(upper, mul(weight, came_b), weight)
            later = jnp.where(upper, total[:, half:], came_b)
            earlier = jnp.where(upper, came, total)
            add = jnp.where(upper, total[:, :half], came_e)
            made = mul(later, earlier)
            total = jnp.concatenate([made[:, :half] + add, made[:, half:]], 1)
        distance *= 2
    return solved, found


def solution(mesh):
    return jax.shard_map(
        on_device,
        mesh=mesh,
        in_specs=(
            P(("groups", "pcol", "prow"), None, None),
            P(("groups", "pcol", "prow"), None),
            P(None, ("groups", "pcol", "prow")),
            P(("groups", "pcol", "prow")),
            P(("groups", "pcol"), None, None),
            P(("groups", "pcol"), None, None),
            P(("groups", "pcol"), "prow"),
        ),
        out_specs=(P(("groups", "pcol", "prow"), None), P(("groups", "pcol"), "prow")),
        check_vma=False,
    )
```

time: 94.8 us -> 29.6 us (0.31)
  blocking collectives: 65.1 us -> 0 us
  between operations: 14.1 us -> 0.87 us
  waiting for transfers between devices: 2.73 us -> 12.6 us
  starting transfers between devices: 5.03 us -> 9.53 us
  matrix products: 5.38 us -> 3.83 us
    all_gather x2 -> x0, blocking collectives: 65.1 us -> none  [entering(): gathered = jax.tree.map(lambda a: lax.all_gather(a, axis), part)]
    ppermute x1 -> x5, waiting for transfers between devices: 2.71 us -> 12.6 us  [the longest x3 11.1 us: on_device(): came = lax.ppermute(total[:, :half] if last else total, 'pcol', pairs)]
    ppermute x1 -> x5, starting transfers between devices: 4.99 us -> 9.53 us  [the longest x1 5.59 us: on_device(): lax.ppermute(sep_coupling[0], 'pcol', [(i, (i - 1) % columns) for i in ra...]
    dot_general x6 -> x11, matrix products: 5.38 us -> 3.83 us  [the longest x9 1.77 us: mul(): return jnp.dot(a, b, precision=lax.Precision.HIGH)]
  transfers between devices with their start and end apart: 2 -> 5, of which waited for: 1 -> 4; matrix products, arithmetic and copies ran while one was open for 0% -> 4% of each run, Pallas kernels for 0% -> 0%
where the time goes in v1:
time: 29.6 us; the launch traced here: 29.4 us
  waiting for transfers between devices  12.6 us (43%)
  starting transfers between devices  9.53 us (32%)
  matrix products  3.83 us (13%)
  local copies, waits for them, and re-layouts  1.68 us (6%)
  other arithmetic  0.94 us (3%)
  between operations  0.87 us (3%)
    ppermute x3, waiting for transfers between devices, on_device(): came = lax.ppermute(total[:, :half] if last else total, 'pcol', pairs)  11.1 us
    ppermute x1, starting transfers between devices, on_device(): lax.ppermute(sep_coupling[0], 'pcol', [(i, (i - 1) % columns) for i in ra...  5.59 us
    ppermute x3, starting transfers between devices, on_device(): came = lax.ppermute(total[:, :half] if last else total, 'pcol', pairs)  3.42 us
    dot_general x9, matrix products, mul(): return jnp.dot(a, b, precision=lax.Precision.HIGH)  1.77 us
    unnamed x15, local copies, waits for them, and re-layouts  1.61 us
    dot_general x1, matrix products, on_device(): jnp.einsum('jab,jbr->jar', leaf_inverse, leaf_rhs.reshape(count, block, w...  1.52 us
    ppermute x1, waiting for transfers between devices, on_device(): lax.ppermute(sep_coupling[0], 'pcol', [(i, (i - 1) % columns) for i in ra...  1.47 us
    eq x1, other arithmetic, on_device(): link == 0  0.75 us
  transfers between devices with their start and end apart: 5, of which 4 were waited for; matrix products, arithmetic and copies ran while one was open for 4% of the time, Pallas kernels for 0%

profile of v1, /device:TPU:0, one launch (start us, length us, event | category | flops | bytes accessed | tf_op | source)
XLA Modules:
  0.0 29.4 jit_solution(8608742696861315383)
XLA Ops:
  0.6 0.0 copy-start
  0.6 0.7 %broadcast_compare_fusion.1 = (pred[16]{0:T(512)(128)(4,1)S(1)}, pred[16]{0:T(512)(128)(4,1)S(1)}) fusion(s32[16]{0:T(128)} %param.10), kind=kLoop, calls=%fused_computation.55 | loop fusion | flops 32 | bytes 96 | tf_op jit(solution)/shard_map/eq | solution.py:30
  1.4 0.1 broadcast_bitcast_fusion
  1.5 0.4 %copy-done = bf16[2048,256]{1,0:T(8,128)(2,1)S(1)} copy-done((bf16[2048,256]{1,0:T(8,128)(2,1)S(1)}, bf16[2048,256]{1,0:T(8,128)(2,1)}, u32[]{:S(2)}) %copy-start) | copy-done | bytes 1048600
  1.9 1.5 %convolution_convert_fusion = bf16[16,128,256]{2,1,0:T(8,128)(2,1)S(1)} fusion(bf16[16,128,128]{2,1,0:T(8,128)(2,1)} %param.7, bf16[16,128,256]{2,1,0:T(8,128)(2,1)S(1)} %bitcast.41), kind=kOutput, calls=%fused_computation | convolution fusion | flops 134742016 | bytes 2621440 | tf_op jit(solution)/shard_map/jab,jbr->jar/dot_general | solution.py:20
  3.4 0.0 copy-start.1
  3.4 0.1 broadcast_select_fusion.1
  3.5 0.0 copy-start.5
  3.5 0.0 copy-start.4
  3.6 0.5 %fusion.5 = f32[256,256]{0,1:T(8,128)S(1)} fusion(bf16[2048,256]{1,0:T(8,128)(2,1)S(1)} %bitcast.42, bf16[128,2048]{1,0:T(8,128)(2,1)S(1)} %get-tuple-element.5, bf16[128,2048]{1,0:T(8,128)(2,1)S(1)} %get-tuple-element.4), kind=kOutput, calls=%fused_computation.14 | convolution fusion | flops 270532608 | bytes 2359296 | tf_op jit(solution)/shard_map/dot_general | solution.py:32
  4.1 0.3 copy-done.1
  4.4 0.5 %collective-permute-start = (f32[256,128]{0,1:T(8,128)S(1)}, f32[256,128]{0,1:T(8,128)S(1)}, u32[]{:S(2)}, u32[]{:S(2)}) collective-permute-start(f32[256,128]{0,1:T(8,128)S(1)} %slice_select_fusion), channel_id=1, source_target_pairs={{0,1},{1,0},{2,3},{3,2},{4,5},{5,4},{6,7},{7,6},{8,9},{9,8},{10,11... | collective-permute-start | bytes 393224 | tf_op jit(solution)/shard_map/ppermute | solution.py:37
  4.9 5.6 %collective-permute-start.1 = (f32[128,128]{1,0:T(8,128)S(1)}, f32[128,128]{1,0:T(8,128)S(1)}, u32[]{:S(2)}, u32[]{:S(2)}) collective-permute-start(f32[128,128]{1,0:T(8,128)S(1)} %bitcast.44), channel_id=1, source_target_pairs={{0,14},{2,0},{4,2},{6,4},{8,6},{10,8},{12,10},{14,12},{1,15},{3,1}... | collective-permute-start | bytes 196616 | tf_op jit(solution)/shard_map/ppermute | solution.py:18
  10.5 0.1 copy.9
  10.6 0.1 copy.10
  10.8 0.2 convolution_bitcast_fusion.3
  11.0 1.5 %collective-permute-done.1 = f32[128,128]{1,0:T(8,128)S(1)} collective-permute-done((f32[128,128]{1,0:T(8,128)S(1)}, f32[128,128]{1,0:T(8,128)S(1)}, u32[]{:S(2)}, u32[]{:S(2)}) %collective-permute-start.1) | collective-permute-done | bytes 65568 | tf_op jit(solution)/shard_map/ppermute | solution.py:18
  12.5 0.2 convolution_bitcast_fusion
  12.7 0.4 %collective-permute-start.2 = (f32[128,256]{0,1:T(8,128)S(1)}, f32[128,256]{0,1:T(8,128)S(1)}, u32[]{:S(2)}, u32[]{:S(2)}) collective-permute-start(f32[128,256]{0,1:T(8,128)S(1)} %pad_maximum_fusion.1), channel_id=1, source_target_pairs={{0,2},{2,0},{4,6},{6,4},{8,10},{10,8},{12,14},{14,12},{1,3},{3,1},... | collective-permute-start | bytes 393224 | tf_op jit(solution)/shard_map/ppermute | solution.py:48
  13.2 4.6 %collective-permute-done.2 = f32[128,256]{0,1:T(8,128)S(1)} collective-permute-done((f32[128,256]{0,1:T(8,128)S(1)}, f32[128,256]{0,1:T(8,128)S(1)}, u32[]{:S(2)}, u32[]{:S(2)}) %collective-permute-start.2) | collective-permute-done | bytes 131104 | tf_op jit(solution)/shard_map/ppermute | solution.py:48
  17.8 0.2 fusion.12
  18.0 0.3 %collective-permute-start.3 = (f32[128,256]{0,1:T(8,128)S(1)}, f32[128,256]{0,1:T(8,128)S(1)}, u32[]{:S(2)}, u32[]{:S(2)}) collective-permute-start(f32[128,256]{0,1:T(8,128)S(1)} %pad_maximum_fusion), channel_id=1, source_target_pairs={{0,4},{2,6},{4,0},{6,2},{8,12},{10,14},{12,8},{14,10},{1,5},{3,7},... | collective-permute-start | bytes 393224 | tf_op jit(solution)/shard_map/ppermute | solution.py:48
  18.4 0.2 fusion.2
  18.6 0.2 fusion.4
  18.8 4.3 %collective-permute-done.3 = f32[128,256]{0,1:T(8,128)S(1)} collective-permute-done((f32[128,256]{0,1:T(8,128)S(1)}, f32[128,256]{0,1:T(8,128)S(1)}, u32[]{:S(2)}, u32[]{:S(2)}) %collective-permute-start.3) | collective-permute-done | bytes 131104 | tf_op jit(solution)/shard_map/ppermute | solution.py:48
  23.1 0.2 convolution_add_fusion
  23.3 2.7 %collective-permute-start.4 = (f32[128,128]{0,1:T(8,128)S(1)}, f32[128,128]{0,1:T(8,128)S(1)}, u32[]{:S(2)}, u32[]{:S(2)}) collective-permute-start(f32[128,128]{0,1:T(8,128)S(1)} %convolution_add_fusion), channel_id=1, source_target_pairs={{0,8},{2,10},{4,12},{6,14},{8,0},{10,2},{12,4},{14,6},{1,9},{3,11}... | collective-permute-start | bytes 196616 | tf_op jit(solution)/shard_map/ppermute | solution.py:48
  25.9 0.2 fusion.1
  26.1 0.2 convolution_select_fusion
  26.3 2.2 %collective-permute-done.4 = f32[128,128]{0,1:T(8,128)S(1)} collective-permute-done((f32[128,128]{0,1:T(8,128)S(1)}, f32[128,128]{0,1:T(8,128)S(1)}, u32[]{:S(2)}, u32[]{:S(2)}) %collective-permute-start.4) | collective-permute-done | bytes 65568 | tf_op jit(solution)/shard_map/ppermute | solution.py:48
  28.5 0.2 fusion
  28.7 0.7 %copy.15 = f32[128,128]{1,0:T(8,128)} copy(f32[128,128]{0,1:T(8,128)S(1)} %fusion) | data formatting | bytes 131072
  (14 shorter events, 0.1 us)
Async XLA Ops:
  0.6 1.2 %copy-start = (bf16[2048,256]{1,0:T(8,128)(2,1)S(1)}, bf16[2048,256]{1,0:T(8,128)(2,1)}, u32[]{:S(2)}) copy-start(bf16[2048,256]{1,0:T(8,128)(2,1)} %param.8) | copy-start | bytes 3145732
  1.9 1.5 %copy-start.3 = (bf16[128,2048]{1,0:T(8,128)(2,1)S(1)}, bf16[128,2048]{1,0:T(8,128)(2,1)}, u32[]{:S(2)}) copy-start(bf16[128,2048]{1,0:T(8,128)(2,1)} %param.9) | copy-start | bytes 1572868
  3.4 1.0 %copy-start.1 = (bf16[16,128,256]{2,1,0:T(8,128)(2,1)}, bf16[16,128,256]{2,1,0:T(8,128)(2,1)S(1)}, u32[]{:S(2)}) copy-start(bf16[16,128,256]{2,1,0:T(8,128)(2,1)S(1)} %convolution_convert_fusion) | copy-start | bytes 3145732
  3.5 1.4 %copy-start.5 = (f32[1,128,128]{2,1,0:T(8,128)S(1)}, f32[1,128,128]{2,1,0:T(8,128)}, u32[]{:S(2)}) copy-start(f32[1,128,128]{2,1,0:T(8,128)} %param.12) | copy-start | bytes 196612
  3.5 7.0 %copy-start.4 = (f32[128,128]{1,0:T(8,128)S(1)}, f32[128,128]{1,0:T(8,128)}, u32[]{:S(2)}) copy-start(f32[128,128]{1,0:T(8,128)} %param.13) | copy-start | bytes 196612
  3.5 7.1 %copy-start.2 = (f32[1,128,128]{2,1,0:T(8,128)S(1)}, f32[1,128,128]{2,1,0:T(8,128)}, u32[]{:S(2)}) copy-start(f32[1,128,128]{2,1,0:T(8,128)} %param.11) | copy-start | bytes 196612
  4.4 6.3 %collective-permute-start = (f32[256,128]{0,1:T(8,128)S(1)}, f32[256,128]{0,1:T(8,128)S(1)}, u32[]{:S(2)}, u32[]{:S(2)}) collective-permute-start(f32[256,128]{0,1:T(8,128)S(1)} %slice_select_fusion), channel_id=1, source_target_pairs={{0,1},{1,0},{2,3},{3,2},{4,5},{5,4},{6,7},{7,6},{8,9},{9,8},{10,11... | collective-permute-start | bytes 393224 | tf_op jit(solution)/shard_map/ppermute | solution.py:37
  4.9 7.5 %collective-permute-start.1 = (f32[128,128]{1,0:T(8,128)S(1)}, f32[128,128]{1,0:T(8,128)S(1)}, u32[]{:S(2)}, u32[]{:S(2)}) collective-permute-start(f32[128,128]{1,0:T(8,128)S(1)} %bitcast.44), channel_id=1, source_target_pairs={{0,14},{2,0},{4,2},{6,4},{8,6},{10,8},{12,10},{14,12},{1,15},{3,1}... | collective-permute-start | bytes 196616 | tf_op jit(solution)/shard_map/ppermute | solution.py:18
  12.7 5.0 %collective-permute-start.2 = (f32[128,256]{0,1:T(8,128)S(1)}, f32[128,256]{0,1:T(8,128)S(1)}, u32[]{:S(2)}, u32[]{:S(2)}) collective-permute-start(f32[128,256]{0,1:T(8,128)S(1)} %pad_maximum_fusion.1), channel_id=1, source_target_pairs={{0,2},{2,0},{4,6},{6,4},{8,10},{10,8},{12,14},{14,12},{1,3},{3,1},... | collective-permute-start | bytes 393224 | tf_op jit(solution)/shard_map/ppermute | solution.py:48
  18.0 5.0 %collective-permute-start.3 = (f32[128,256]{0,1:T(8,128)S(1)}, f32[128,256]{0,1:T(8,128)S(1)}, u32[]{:S(2)}, u32[]{:S(2)}) collective-permute-start(f32[128,256]{0,1:T(8,128)S(1)} %pad_maximum_fusion), channel_id=1, source_target_pairs={{0,4},{2,6},{4,0},{6,2},{8,12},{10,14},{12,8},{14,10},{1,5},{3,7},... | collective-permute-start | bytes 393224 | tf_op jit(solution)/shard_map/ppermute | solution.py:48
  23.3 5.2 %collective-permute-start.4 = (f32[128,128]{0,1:T(8,128)S(1)}, f32[128,128]{0,1:T(8,128)S(1)}, u32[]{:S(2)}, u32[]{:S(2)}) collective-permute-start(f32[128,128]{0,1:T(8,128)S(1)} %convolution_add_fusion), channel_id=1, source_target_pairs={{0,8},{2,10},{4,12},{6,14},{8,0},{10,2},{12,4},{14,6},{1,9},{3,11}... | collective-permute-start | bytes 196616 | tf_op jit(solution)/shard_map/ppermute | solution.py:48

commit v2 on v1

v2 whole, which is shorter than its diff:
```python
import jax
import jax.numpy as jnp
from jax import lax
from jax.experimental import pallas as pl
from jax.experimental.pallas import tpu as pltpu
from jax.sharding import PartitionSpec as P

VMEM = pl.BlockSpec(memory_space=pltpu.VMEM)
ANY = pl.BlockSpec(memory_space=pl.ANY)
CHUNKS = 4


def mul(a, b):
    return jnp.dot(a, b, precision=lax.Precision.HIGH)


def leaf_kernel(
    parent_in, inverse_in, rhs_in, coupling_in, right_in, sep_in,
    solved_out, kept, sent, sep_out,
    parent, inverse, rhs, coupling, right, solved, both, sems,
):
    link = pltpu.make_async_copy(parent_in, parent, sems.at[CHUNKS, 3])
    link.start()
    count, block, _ = inverse.shape
    half = kept.shape[1]
    step = count // CHUNKS
    copies = []
    for c in range(CHUNKS):
        leaves = pl.ds(c * step, step)
        rows = pl.ds(c * step * block, step * block)
        copies.append(
            (
                pltpu.make_async_copy(inverse_in.at[leaves], inverse.at[leaves], sems.at[c, 0]),
                pltpu.make_async_copy(rhs_in.at[rows], rhs.at[rows], sems.at[c, 1]),
            )
        )
        for copy in copies[-1]:
            copy.start()
    rest = [
        pltpu.make_async_copy(coupling_in, coupling, sems.at[CHUNKS, 0]),
        pltpu.make_async_copy(right_in, right, sems.at[CHUNKS, 1]),
        pltpu.make_async_copy(sep_in, sep_out, sems.at[CHUNKS, 2]),
    ]
    for copy in rest:
        copy.start()
    outs = []
    for c in range(CHUNKS):
        for copy in copies[c]:
            copy.wait()
        for j in range(c * step, (c + 1) * step):
            rows = pl.ds(j * block, block)
            solved[rows, :] = jnp.dot(
                inverse[j], rhs[rows, :], preferred_element_type=jnp.float32
            ).astype(jnp.bfloat16)
        rows = pl.ds(c * step * block, step * block)
        outs.append(pltpu.make_async_copy(solved.at[rows], solved_out.at[rows], sems.at[c, 2]))
        outs[-1].start()
    link.wait()
    rest[0].wait()
    for j in range(count):
        columns = pl.ds(j * block, block)
        piece = coupling[:, columns]
        zero = jnp.zeros_like(piece)
        both[pl.ds(0, block), columns] = jnp.where(parent[j] == 0, piece, zero)
        both[pl.ds(block, block), columns] = jnp.where(parent[j] == 1, piece, zero)
    sums = jnp.dot(both[...], solved[...], preferred_element_type=jnp.float32)
    first = lax.axis_index("prow") == 0
    sent[...] = jnp.where(first, sums[:, half:], sums[:, :half])
    mine = jnp.where(first, sums[:, :half], sums[:, half:])
    rest[1].wait()
    kept[pl.ds(0, block), :] = mine[:block] - right[...]
    kept[pl.ds(block, block), :] = mine[block:]
    rest[2].wait()
    for out in outs:
        out.wait()


def leaves(parent, inverse, rhs, coupling, right, sep):
    count, block, _ = inverse.shape
    width = rhs.shape[1]
    share = pltpu.VMEM((2 * block, width // 2), jnp.float32)
    return pl.pallas_call(
        leaf_kernel,
        out_shape=(jax.ShapeDtypeStruct(rhs.shape, jnp.bfloat16), share, share, pltpu.VMEM(sep.shape, sep.dtype)),
        in_specs=[ANY] * 6,
        out_specs=(ANY, VMEM, VMEM, VMEM),
        scratch_shapes=[
            pltpu.SMEM(parent.shape, parent.dtype),
            pltpu.VMEM(inverse.shape, inverse.dtype),
            pltpu.VMEM(rhs.shape, rhs.dtype),
            pltpu.VMEM(coupling.shape, coupling.dtype),
            pltpu.VMEM(right.shape, right.dtype),
            pltpu.VMEM(rhs.shape, jnp.bfloat16),
            pltpu.VMEM((2 * block, count * block), jnp.bfloat16),
            pltpu.SemaphoreType.DMA((CHUNKS + 1, 4)),
        ],
        compiler_params=pltpu.CompilerParams(vmem_limit_bytes=16 * 2**20),
    )(*[pltpu.with_memory_space_constraint(a, pltpu.HBM) for a in (parent, inverse, rhs, coupling, right, sep)])


def on_device(leaf_inverse, leaf_rhs, leaf_coupling, parent, sep_inverse, sep_coupling, sep_rhs):
    block = leaf_inverse.shape[1]
    half = leaf_rhs.shape[1] // 2
    columns = lax.axis_size("pcol")
    column = lax.axis_index("pcol")
    ahead = lax.ppermute(sep_coupling[0], "pcol", [(i, i - 1) for i in range(1, columns)])
    solved, kept, sent, inverse = leaves(
        parent, leaf_inverse, leaf_rhs, leaf_coupling, sep_rhs, sep_inverse[0]
    )
    b = -mul(ahead, inverse)
    came = lax.ppermute(sent, "prow", [(0, 1), (1, 0)])
    b, kept = lax.optimization_barrier((b, kept))
    sums = kept + came
    minus, onward = sums[:block], sums[block:]
    weight = inverse
    found = -mul(inverse, minus)
    total = jnp.concatenate([mul(b, minus) + onward, b], 1)
    distance = 1
    while distance < columns:
        last = 2 * distance >= columns
        pairs = [(i, i ^ distance) for i in range(columns) if i ^ distance < columns]
        came = lax.ppermute(total[:, :half] if last else total, "pcol", pairs)
        upper = (column & distance) != 0
        came_e = came[:, :half]
        found = jnp.where(upper, found - mul(weight, came_e), found)
        if not last:
            came_b = came[:, half:]
            weight = jnp.where(upper, mul(weight, came_b), weight)
            later = jnp.where(upper, total[:, half:], came_b)
            earlier = jnp.where(upper, came, total)
            add = jnp.where(upper, total[:, :half], came_e)
            made = mul(later, earlier)
            total = jnp.concatenate([made[:, :half] + add, made[:, half:]], 1)
        distance *= 2
    return solved, found
def solution(mesh):
    return jax.shard_map(
        on_device,
        mesh=mesh,
        in_specs=(
            P(("groups", "pcol", "prow"), None, None),
            P(("groups", "pcol", "prow"), None),
            P(None, ("groups", "pcol", "prow")),
            P(("groups", "pcol", "prow")),
            P(("groups", "pcol"), None, None),
            P(("groups", "pcol"), None, None),
            P(("groups", "pcol"), "prow"),
        ),
        out_specs=(P(("groups", "pcol", "prow"), None), P(("groups", "pcol"), "prow")),
        check_vma=False,
    )
```

time: 29.6 us -> 26.8 us (0.905)
  Pallas kernels: 0 us -> 2.77 us
  waiting for transfers between devices: 12.6 us -> 9.95 us
  local copies, waits for them, and re-layouts: 1.68 us -> 0 us
  matrix products: 3.83 us -> 2.43 us
  starting transfers between devices: 9.53 us -> 10.6 us
  other arithmetic: 0.94 us -> 0.06 us
    ppermute x3, starting transfers between devices: 3.42 us -> 8.81 us  [on_device(): came = lax.ppermute(total[:, :half] if last else total, 'pcol', pairs)]
    ppermute x2, starting transfers between devices: 6.11 us -> 1.82 us  [the longest x1 1.29 us: on_device(): lax.ppermute(sep_coupling[0], 'pcol', [(i, i - 1) for i in range(1, colum...]
    ppermute x3, waiting for transfers between devices: 11.1 us -> 7.25 us  [on_device(): came = lax.ppermute(total[:, :half] if last else total, 'pcol', pairs)]
    pallas_call x0 -> x1, Pallas kernels: none -> 2.77 us  [leaves(): pl.pallas_call(leaf_kernel, out_shape=(jax.ShapeDtypeStruct(rhs.shape, jn...]
    dot_general x2 -> x0, matrix products: 2.06 us -> none  [the longest x1 1.52 us: on_device(): jnp.einsum('jab,jbr->jar', leaf_inverse, leaf_rhs.reshape(count, block, w...]
    unnamed x15 -> x0, local copies, waits for them, and re-layouts: 1.61 us -> none
    ppermute x2, waiting for transfers between devices: 1.48 us -> 2.69 us  [the longest x1 2.69 us: on_device(): lax.ppermute(sep_coupling[0], 'pcol', [(i, i - 1) for i in range(1, colum...]
    eq x1 -> x0, other arithmetic: 0.75 us -> none  [on_device(): link == 0]
  transfers between devices with their start and end apart: 5 -> 5, of which waited for: 4 -> 4; matrix products, arithmetic and copies ran while one was open for 4% -> 4% of each run, Pallas kernels for 0% -> 10%
where the time goes in v2:
time: 26.8 us; the launch traced here: 26.6 us
  starting transfers between devices  10.6 us (40%)
  waiting for transfers between devices  9.95 us (37%)
  Pallas kernels  2.77 us (10%)
  matrix products  2.43 us (9%)
  between operations  0.76 us (3%)
    ppermute x3, starting transfers between devices, on_device(): came = lax.ppermute(total[:, :half] if last else total, 'pcol', pairs)  8.81 us
    ppermute x3, waiting for transfers between devices, on_device(): came = lax.ppermute(total[:, :half] if last else total, 'pcol', pairs)  7.25 us
    pallas_call x1, Pallas kernels, leaves(): pl.pallas_call(leaf_kernel, out_shape=(jax.ShapeDtypeStruct(rhs.shape, jn...  2.77 us
    ppermute x1, waiting for transfers between devices, on_device(): lax.ppermute(sep_coupling[0], 'pcol', [(i, i - 1) for i in range(1, colum...  2.69 us
    dot_general x10, matrix products, mul(): return jnp.dot(a, b, precision=lax.Precision.HIGH)  2.43 us
    ppermute x1, starting transfers between devices, on_device(): lax.ppermute(sep_coupling[0], 'pcol', [(i, i - 1) for i in range(1, colum...  1.29 us
  transfers between devices with their start and end apart: 5, of which 4 were waited for; matrix products, arithmetic and copies ran while one was open for 4% of the time, Pallas kernels for 10%

profile of v2, /device:TPU:0, one launch (start us, length us, event | category | flops | bytes accessed | tf_op | source)
XLA Modules:
  0.0 26.6 jit_solution(13005430074825344638)
XLA Ops:
  0.6 1.3 %collective-permute-start = (f32[128,128]{1,0:T(8,128)}, f32[128,128]{1,0:T(8,128)S(1)}, u32[]{:S(2)}, u32[]{:S(2)}) collective-permute-start(f32[128,128]{1,0:T(8,128)} %bitcast.15), channel_id=1, source_target_pairs={{2,0},{4,2},{6,4},{8,6},{10,8},{12,10},{14,12},{3,1},{5,3},{7,5},{... | collective-permute-start | bytes 196616 | tf_op jit(solution)/shard_map/ppermute | solution.py:106
  1.9 2.8 %shard_map.86 = (bf16[2048,256]{1,0:T(8,128)(2,1)}, f32[256,128]{1,0:T(8,128)S(1)}, f32[256,128]{1,0:T(8,128)S(1)}, f32[128,128]{1,0:T(8,128)S(1)}) custom-call(s32[16]{0:T(128)} %parent_in.1, bf16[16,128,128]{2,1,0:T(8,128)(2,1)} %inverse_in.1, bf16[2048,256]{1,0:T(8,128)(2,1)} %rhs_in.1, bf16[128,2048]{1,0:T(8,128)(2,1)} %coupling_in.1, ...), custom_call_target="tpu_custom_call" | custom-call | tf_op jit(solution)/shard_map/pallas_call | solution.py:82
  4.7 0.5 %collective-permute-start.1 = (f32[256,128]{1,0:T(8,128)S(1)}, f32[256,128]{1,0:T(8,128)S(1)}, u32[]{:S(2)}, u32[]{:S(2)}) collective-permute-start(f32[256,128]{1,0:T(8,128)S(1)} %get-tuple-element.12), channel_id=1, source_target_pairs={{0,1},{1,0},{2,3},{3,2},{4,5},{5,4},{6,7},{7,6},{8,9},{9,8},{10,11... | collective-permute-start | bytes 393224 | tf_op jit(solution)/shard_map/ppermute | solution.py:111
  5.2 2.7 %collective-permute-done = f32[128,128]{1,0:T(8,128)S(1)} collective-permute-done((f32[128,128]{1,0:T(8,128)}, f32[128,128]{1,0:T(8,128)S(1)}, u32[]{:S(2)}, u32[]{:S(2)}) %collective-permute-start) | collective-permute-done | bytes 65568 | tf_op jit(solution)/shard_map/ppermute | solution.py:106
  7.9 0.2 fusion.3
  8.1 0.0 collective-permute-done.1
  8.1 0.2 convolution_add_fusion.1
  8.3 3.0 %collective-permute-start.2 = (f32[128,256]{1,0:T(8,128)S(1)}, f32[128,256]{1,0:T(8,128)S(1)}, u32[]{:S(2)}, u32[]{:S(2)}) collective-permute-start(f32[128,256]{1,0:T(8,128)S(1)} %pad_maximum_fusion.1), channel_id=1, source_target_pairs={{0,2},{2,0},{4,6},{6,4},{8,10},{10,8},{12,14},{14,12},{1,3},{3,1},... | collective-permute-start | bytes 393224 | tf_op jit(solution)/shard_map/ppermute | solution.py:122
  11.3 0.2 convolution_negate_fusion
  11.5 2.8 %collective-permute-done.2 = f32[128,256]{1,0:T(8,128)S(1)} collective-permute-done((f32[128,256]{1,0:T(8,128)S(1)}, f32[128,256]{1,0:T(8,128)S(1)}, u32[]{:S(2)}, u32[]{:S(2)}) %collective-permute-start.2) | collective-permute-done | bytes 131104 | tf_op jit(solution)/shard_map/ppermute | solution.py:122
  14.3 0.2 fusion.4
  14.5 2.8 %collective-permute-start.3 = (f32[128,256]{1,0:T(8,128)S(1)}, f32[128,256]{1,0:T(8,128)S(1)}, u32[]{:S(2)}, u32[]{:S(2)}) collective-permute-start(f32[128,256]{1,0:T(8,128)S(1)} %pad_maximum_fusion), channel_id=1, source_target_pairs={{0,4},{2,6},{4,0},{6,2},{8,12},{10,14},{12,8},{14,10},{1,5},{3,7},... | collective-permute-start | bytes 393224 | tf_op jit(solution)/shard_map/ppermute | solution.py:122
  17.3 0.2 fusion.2
  17.5 0.2 convolution_select_fusion.1
  17.7 2.6 %collective-permute-done.3 = f32[128,256]{1,0:T(8,128)S(1)} collective-permute-done((f32[128,256]{1,0:T(8,128)S(1)}, f32[128,256]{1,0:T(8,128)S(1)}, u32[]{:S(2)}, u32[]{:S(2)}) %collective-permute-start.3) | collective-permute-done | bytes 131104 | tf_op jit(solution)/shard_map/ppermute | solution.py:122
  20.3 0.2 convolution_add_fusion
  20.5 3.1 %collective-permute-start.4 = (f32[128,128]{1,0:T(8,128)S(1)}, f32[128,128]{1,0:T(8,128)S(1)}, u32[]{:S(2)}, u32[]{:S(2)}) collective-permute-start(f32[128,128]{1,0:T(8,128)S(1)} %convolution_add_fusion), channel_id=1, source_target_pairs={{0,8},{2,10},{4,12},{6,14},{8,0},{10,2},{12,4},{14,6},{1,9},{3,11}... | collective-permute-start | bytes 196616 | tf_op jit(solution)/shard_map/ppermute | solution.py:122
  23.5 0.2 fusion.1
  23.7 0.2 convolution_select_fusion
  23.9 1.9 %collective-permute-done.4 = f32[128,128]{1,0:T(8,128)S(1)} collective-permute-done((f32[128,128]{1,0:T(8,128)S(1)}, f32[128,128]{1,0:T(8,128)S(1)}, u32[]{:S(2)}, u32[]{:S(2)}) %collective-permute-start.4) | collective-permute-done | bytes 65568 | tf_op jit(solution)/shard_map/ppermute | solution.py:122
  25.8 0.8 %fusion = f32[128,128]{1,0:T(8,128)} fusion(f32[128,128]{1,0:T(8,128)S(1)} %fusion.1, f32[128,128]{1,0:T(8,128)S(1)} %convolution_select_fusion, f32[128,128]{1,0:T(8,128)S(1)} %collective-permute-done.4, pred[]{:T(512)S(6)} %ne.9), kind=kOutput, calls=%fused_computation.4 | convolution fusion | flops 12615680 | bytes 262145 | tf_op jit(solution)/shard_map/dot_general | solution.py:14
  (4 shorter events, 0.1 us)
Async XLA Ops:
  0.6 7.3 %collective-permute-start = (f32[128,128]{1,0:T(8,128)}, f32[128,128]{1,0:T(8,128)S(1)}, u32[]{:S(2)}, u32[]{:S(2)}) collective-permute-start(f32[128,128]{1,0:T(8,128)} %bitcast.15), channel_id=1, source_target_pairs={{2,0},{4,2},{6,4},{8,6},{10,8},{12,10},{14,12},{3,1},{5,3},{7,5},{... | collective-permute-start | bytes 196616 | tf_op jit(solution)/shard_map/ppermute | solution.py:106
  4.7 3.4 %collective-permute-start.1 = (f32[256,128]{1,0:T(8,128)S(1)}, f32[256,128]{1,0:T(8,128)S(1)}, u32[]{:S(2)}, u32[]{:S(2)}) collective-permute-start(f32[256,128]{1,0:T(8,128)S(1)} %get-tuple-element.12), channel_id=1, source_target_pairs={{0,1},{1,0},{2,3},{3,2},{4,5},{5,4},{6,7},{7,6},{8,9},{9,8},{10,11... | collective-permute-start | bytes 393224 | tf_op jit(solution)/shard_map/ppermute | solution.py:111
  8.3 5.9 %collective-permute-start.2 = (f32[128,256]{1,0:T(8,128)S(1)}, f32[128,256]{1,0:T(8,128)S(1)}, u32[]{:S(2)}, u32[]{:S(2)}) collective-permute-start(f32[128,256]{1,0:T(8,128)S(1)} %pad_maximum_fusion.1), channel_id=1, source_target_pairs={{0,2},{2,0},{4,6},{6,4},{8,10},{10,8},{12,14},{14,12},{1,3},{3,1},... | collective-permute-start | bytes 393224 | tf_op jit(solution)/shard_map/ppermute | solution.py:122
  14.5 5.8 %collective-permute-start.3 = (f32[128,256]{1,0:T(8,128)S(1)}, f32[128,256]{1,0:T(8,128)S(1)}, u32[]{:S(2)}, u32[]{:S(2)}) collective-permute-start(f32[128,256]{1,0:T(8,128)S(1)} %pad_maximum_fusion), channel_id=1, source_target_pairs={{0,4},{2,6},{4,0},{6,2},{8,12},{10,14},{12,8},{14,10},{1,5},{3,7},... | collective-permute-start | bytes 393224 | tf_op jit(solution)/shard_map/ppermute | solution.py:122
  20.5 5.3 %collective-permute-start.4 = (f32[128,128]{1,0:T(8,128)S(1)}, f32[128,128]{1,0:T(8,128)S(1)}, u32[]{:S(2)}, u32[]{:S(2)}) collective-permute-start(f32[128,128]{1,0:T(8,128)S(1)} %convolution_add_fusion), channel_id=1, source_target_pairs={{0,8},{2,10},{4,12},{6,14},{8,0},{10,2},{12,4},{14,6},{1,9},{3,11}... | collective-permute-start | bytes 196616 | tf_op jit(solution)/shard_map/ppermute | solution.py:122

commit v3 on v2

v3 whole, which is shorter than its diff:
```python
import functools

import jax
import jax.numpy as jnp
from jax import lax
from jax.experimental import pallas as pl
from jax.experimental.pallas import tpu as pltpu
from jax.sharding import PartitionSpec as P

VMEM = pl.BlockSpec(memory_space=pltpu.VMEM)
ANY = pl.BlockSpec(memory_space=pl.ANY)
CHUNKS = 2


def mul(a, b):
    return jnp.dot(a, b, precision=lax.Precision.HIGH)


def leaf_kernel(
    parent_in, inverse_in, rhs_in, coupling_in, right_in, sep_in,
    solved, kept, sent, sep_out,
    parent, inverse, rhs, coupling, right, both, sems,
):
    count, block, _ = inverse.shape
    half = kept.shape[1]
    step = count // CHUNKS
    first_copies = [
        pltpu.make_async_copy(parent_in, parent, sems.at[CHUNKS, 0]),
        pltpu.make_async_copy(coupling_in, coupling, sems.at[CHUNKS, 1]),
    ]
    chunk_copies = []
    for c in range(CHUNKS):
        leaves = pl.ds(c * step, step)
        rows = pl.ds(c * step * block, step * block)
        chunk_copies.append(
            [
                pltpu.make_async_copy(inverse_in.at[leaves], inverse.at[leaves], sems.at[c, 0]),
                pltpu.make_async_copy(rhs_in.at[rows], rhs.at[rows], sems.at[c, 1]),
            ]
        )
    last_copies = [
        pltpu.make_async_copy(right_in, right, sems.at[CHUNKS, 2]),
        pltpu.make_async_copy(sep_in, sep_out, sems.at[CHUNKS, 3]),
    ]
    for copy in first_copies + sum(chunk_copies, []) + last_copies:
        copy.start()
    for copy in first_copies:
        copy.wait()
    for j in range(count):
        columns = pl.ds(j * block, block)
        piece = coupling[:, columns]
        zero = jnp.zeros_like(piece)
        both[pl.ds(0, block), columns] = jnp.where(parent[j] == 0, piece, zero)
        both[pl.ds(block, block), columns] = jnp.where(parent[j] == 1, piece, zero)
    sums = None
    for c in range(CHUNKS):
        for copy in chunk_copies[c]:
            copy.wait()
        for j in range(c * step, (c + 1) * step):
            rows = pl.ds(j * block, block)
            solved[rows, :] = jnp.dot(
                inverse[j], rhs[rows, :], preferred_element_type=jnp.float32
            ).astype(jnp.bfloat16)
        rows = pl.ds(c * step * block, step * block)
        part = jnp.dot(both[:, rows], solved[rows, :], preferred_element_type=jnp.float32)
        sums = part if c == 0 else sums + part
    first = lax.axis_index("prow") == 0
    sent[...] = jnp.where(first, sums[:, half:], sums[:, :half])
    mine = jnp.where(first, sums[:, :half], sums[:, half:])
    for copy in last_copies:
        copy.wait()
    kept[pl.ds(0, block), :] = mine[:block] - right[...]
    kept[pl.ds(block, block), :] = mine[block:]


def leaves(parent, inverse, rhs, coupling, right, sep):
    count, block, _ = inverse.shape
    width = rhs.shape[1]
    share = pltpu.VMEM((2 * block, width // 2), jnp.float32)
    return pl.pallas_call(
        leaf_kernel,
        out_shape=(pltpu.VMEM(rhs.shape, jnp.bfloat16), share, share, pltpu.VMEM(sep.shape, sep.dtype)),
        in_specs=[ANY] * 6,
        out_specs=(VMEM, VMEM, VMEM, VMEM),
        scratch_shapes=[
            pltpu.SMEM(parent.shape, parent.dtype),
            pltpu.VMEM(inverse.shape, inverse.dtype),
            pltpu.VMEM(rhs.shape, rhs.dtype),
            pltpu.VMEM(coupling.shape, coupling.dtype),
            pltpu.VMEM(right.shape, right.dtype),
            pltpu.VMEM((2 * block, count * block), jnp.bfloat16),
            pltpu.SemaphoreType.DMA((CHUNKS + 1, 4)),
        ],
        compiler_params=pltpu.CompilerParams(vmem_limit_bytes=16 * 2**20),
    )(*[pltpu.with_memory_space_constraint(a, pltpu.HBM) for a in (parent, inverse, rhs, coupling, right, sep)])


def store_kernel(solved, after, out, sem):
    copy = pltpu.make_async_copy(solved, out, sem)
    copy.start()
    copy.wait()


def store(array, after):
    return pl.pallas_call(
        store_kernel,
        out_shape=pltpu.HBM(array.shape, array.dtype),
        in_specs=[VMEM, ANY],
        out_specs=ANY,
        scratch_shapes=[pltpu.SemaphoreType.DMA],
        cost_estimate=pl.CostEstimate(flops=0, bytes_accessed=2**16, transcendentals=0),
    )(*[pltpu.with_memory_space_constraint(a, pltpu.VMEM) for a in (array, after)])


def split(a):
    high = a.astype(jnp.bfloat16)
    return high, (a - high.astype(jnp.float32)).astype(jnp.bfloat16)


def product(a, b):
    def dot(x, y):
        return jnp.dot(x, y, preferred_element_type=jnp.float32)

    (ah, al), (bh, bl) = split(a), split(b)
    return dot(ah, bh) + (dot(ah, bl) + dot(al, bh))


def finish_kernel(distance, found, weight, came, written, out, result, sem):
    del written

    @pl.when((lax.axis_index("pcol") & distance) != 0)
    def _():
        result[...] = found[...] - product(weight[...], came[...])
        copy = pltpu.make_async_copy(result, out, sem)
        copy.start()
        copy.wait()


def finish(distance, found, weight, came):
    written = store(found, weight)
    return pl.pallas_call(
        functools.partial(finish_kernel, distance),
        out_shape=pltpu.HBM(found.shape, found.dtype),
        in_specs=[VMEM, VMEM, VMEM, ANY],
        out_specs=ANY,
        scratch_shapes=[pltpu.VMEM(found.shape, found.dtype), pltpu.SemaphoreType.DMA],
        input_output_aliases={3: 0},
        cost_estimate=pl.CostEstimate(flops=0, bytes_accessed=2**16, transcendentals=0),
    )(*[pltpu.with_memory_space_constraint(a, pltpu.VMEM) for a in (found, weight, came)], written)


def on_device(leaf_inverse, leaf_rhs, leaf_coupling, parent, sep_inverse, sep_coupling, sep_rhs):
    block = leaf_inverse.shape[1]
    half = leaf_rhs.shape[1] // 2
    columns = lax.axis_size("pcol")
    column = lax.axis_index("pcol")
    ahead = lax.ppermute(sep_coupling[0], "pcol", [(i, i - 1) for i in range(1, columns)])
    solved, kept, sent, inverse = leaves(
        parent, leaf_inverse, leaf_rhs, leaf_coupling, sep_rhs, sep_inverse[0]
    )
    b = -mul(ahead, inverse)
    came = lax.ppermute(sent, "prow", [(0, 1), (1, 0)])
    b, kept = lax.optimization_barrier((b, kept))
    sums = kept + came
    minus, onward = sums[:block], sums[block:]
    weight = inverse
    found = -mul(inverse, minus)
    total = jnp.concatenate([mul(b, minus) + onward, b], 1)
    def join(lower, higher):
        made = mul(higher[:, half:], lower)
        return jnp.concatenate([made[:, :half] + higher[:, :half], made[:, half:]], 1)

    def swap(array, distance):
        pairs = [(i, i ^ distance) for i in range(columns) if i ^ distance < columns]
        return lax.ppermute(array, "pcol", pairs)

    late = []
    distance = 1
    flights = {d: swap(total, d) for d in (1, 2, 3)}
    while distance < columns:
        last = 2 * distance >= columns
        if distance == 1:
            came = flights[1]
        elif distance == 2:
            odd = (column & 1) != 0
            came = join(
                jnp.where(odd, flights[3], flights[2]), jnp.where(odd, flights[2], flights[3])
            )
        else:
            total = total[:, :half] if last else total
            came = swap(total, distance)
        if last:
            late, total_after = lax.optimization_barrier((late, total))
            for above, block_came in late:
                moved = mul(weight, block_came)
                found = jnp.where(above, found - moved[:, :half], found)
                weight = jnp.where(above, moved[:, half:], weight)
            solved = store(solved, total_after)
            found = finish(distance, found, weight, came)
            break
        upper = (column & distance) != 0
        late.append((upper, came))
        total = join(jnp.where(upper, came, total), jnp.where(upper, total, came))
        distance *= 2
    return solved, found
def solution(mesh):
    return jax.shard_map(
        on_device,
        mesh=mesh,
        in_specs=(
            P(("groups", "pcol", "prow"), None, None),
            P(("groups", "pcol", "prow"), None),
            P(None, ("groups", "pcol", "prow")),
            P(("groups", "pcol", "prow")),
            P(("groups", "pcol"), None, None),
            P(("groups", "pcol"), None, None),
            P(("groups", "pcol"), "prow"),
        ),
        out_specs=(P(("groups", "pcol", "prow"), None), P(("groups", "pcol"), "prow")),
        check_vma=False,
    )
```

time: 26.8 us -> 25.5 us (0.951)
  starting transfers between devices: 10.6 us -> 9.02 us
  Pallas kernels: 2.77 us -> 3.99 us
  matrix products: 2.43 us -> 1.53 us
    ppermute x3 -> x4, starting transfers between devices: 8.81 us -> 7.21 us  [swap(): return lax.ppermute(array, 'pcol', pairs)]
    pallas_call x1 -> x4, Pallas kernels: 2.77 us -> 3.99 us  [the longest x1 2.36 us: leaves(): pl.pallas_call(leaf_kernel, out_shape=(pltpu.VMEM(rhs.shape, jnp.bfloat16...]
    dot_general x10 -> x8, matrix products: 2.43 us -> 1.53 us  [mul(): return jnp.dot(a, b, precision=lax.Precision.HIGH)]
    ppermute x3 -> x4, waiting for transfers between devices: 7.25 us -> 6.73 us  [swap(): return lax.ppermute(array, 'pcol', pairs)]
    ppermute x1, waiting for transfers between devices: 2.69 us -> 3.11 us  [on_device(): lax.ppermute(sep_coupling[0], 'pcol', [(i, i - 1) for i in range(1, colum...]
  transfers between devices with their start and end apart: 5 -> 6, of which waited for: 4 -> 5; matrix products, arithmetic and copies ran while one was open for 4% -> 4% of each run, Pallas kernels for 10% -> 16%
where the time goes in v3:
time: 25.5 us; the launch traced here: 25.3 us
  waiting for transfers between devices  9.84 us (39%)
  starting transfers between devices  9.02 us (35%)
  Pallas kernels  3.99 us (16%)
  matrix products  1.53 us (6%)
  between operations  0.79 us (3%)
    ppermute x4, starting transfers between devices, swap(): return lax.ppermute(array, 'pcol', pairs)  7.21 us
    ppermute x4, waiting for transfers between devices, swap(): return lax.ppermute(array, 'pcol', pairs)  6.73 us
    ppermute x1, waiting for transfers between devices, on_device(): lax.ppermute(sep_coupling[0], 'pcol', [(i, i - 1) for i in range(1, colum...  3.11 us
    pallas_call x1, Pallas kernels, leaves(): pl.pallas_call(leaf_kernel, out_shape=(pltpu.VMEM(rhs.shape, jnp.bfloat16...  2.36 us
    pallas_call x2, Pallas kernels, store(): pl.pallas_call(store_kernel, out_shape=pltpu.HBM(array.shape, array.dtype...  1.62 us
    dot_general x8, matrix products, mul(): return jnp.dot(a, b, precision=lax.Precision.HIGH)  1.53 us
    ppermute x1, starting transfers between devices, on_device(): lax.ppermute(sep_coupling[0], 'pcol', [(i, i - 1) for i in range(1, colum...  1.29 us
    ppermute x1, starting transfers between devices, on_device(): came = lax.ppermute(sent, 'prow', [(0, 1), (1, 0)])  0.52 us
  transfers between devices with their start and end apart: 6, of which 5 were waited for; matrix products, arithmetic and copies ran while one was open for 4% of the time, Pallas kernels for 16%

profile of v3, /device:TPU:0, one launch (start us, length us, event | category | flops | bytes accessed | tf_op | source)
XLA Modules:
  0.0 25.3 jit_solution(12574260239379322760)
XLA Ops:
  0.6 1.3 %collective-permute-start = (f32[128,128]{1,0:T(8,128)}, f32[128,128]{1,0:T(8,128)S(1)}, u32[]{:S(2)}, u32[]{:S(2)}) collective-permute-start(f32[128,128]{1,0:T(8,128)} %bitcast.12), channel_id=1, source_target_pairs={{2,0},{4,2},{6,4},{8,6},{10,8},{12,10},{14,12},{3,1},{5,3},{7,5},{... | collective-permute-start | bytes 196616 | tf_op jit(solution)/shard_map/ppermute | solution.py:157
  1.9 2.4 %shard_map.86 = (bf16[2048,256]{1,0:T(8,128)(2,1)S(1)}, f32[256,128]{1,0:T(8,128)S(1)}, f32[256,128]{1,0:T(8,128)S(1)}, f32[128,128]{1,0:T(8,128)S(1)}) custom-call(s32[16]{0:T(128)} %parent_in.1, bf16[16,128,128]{2,1,0:T(8,128)(2,1)} %inverse_in.1, bf16[2048,256]{1,0:T(8,128)(2,1)} %rhs_in.1, bf16[128,2048]{1,0:T(8,128)(2,1)} %coupling_in.1, ...), custom_call_target="tpu_custom_call" | custom-call | tf_op jit(solution)/shard_map/pallas_call | solution.py:80
  4.3 0.5 %collective-permute-start.1 = (f32[256,128]{1,0:T(8,128)S(1)}, f32[256,128]{1,0:T(8,128)S(1)}, u32[]{:S(2)}, u32[]{:S(2)}) collective-permute-start(f32[256,128]{1,0:T(8,128)S(1)} %get-tuple-element.18), channel_id=1, source_target_pairs={{0,1},{1,0},{2,3},{3,2},{4,5},{5,4},{6,7},{7,6},{8,9},{9,8},{10,11... | collective-permute-start | bytes 393224 | tf_op jit(solution)/shard_map/ppermute | solution.py:162
  4.8 3.1 %collective-permute-done = f32[128,128]{1,0:T(8,128)S(1)} collective-permute-done((f32[128,128]{1,0:T(8,128)}, f32[128,128]{1,0:T(8,128)S(1)}, u32[]{:S(2)}, u32[]{:S(2)}) %collective-permute-start) | collective-permute-done | bytes 65568 | tf_op jit(solution)/shard_map/ppermute | solution.py:157
  7.9 0.2 fusion
  8.1 0.0 collective-permute-done.1
  8.1 0.2 convolution_add_fusion.1
  8.3 2.7 %collective-permute-start.3 = (f32[128,256]{1,0:T(8,128)S(1)}, f32[128,256]{1,0:T(8,128)S(1)}, u32[]{:S(2)}, u32[]{:S(2)}) collective-permute-start(f32[128,256]{1,0:T(8,128)S(1)} %pad_maximum_fusion.2), channel_id=1, source_target_pairs={{0,4},{2,6},{4,0},{6,2},{8,12},{10,14},{12,8},{14,10},{1,5},{3,7},... | collective-permute-start | bytes 393224 | tf_op jit(solution)/shard_map/ppermute | solution.py:175
  11.0 1.8 %collective-permute-start.4 = (f32[128,256]{1,0:T(8,128)S(1)}, f32[128,256]{1,0:T(8,128)S(1)}, u32[]{:S(2)}, u32[]{:S(2)}) collective-permute-start(f32[128,256]{1,0:T(8,128)S(1)} %pad_maximum_fusion.2), channel_id=1, source_target_pairs={{0,6},{2,4},{4,2},{6,0},{8,14},{10,12},{12,10},{14,8},{1,7},{3,5},... | collective-permute-start | bytes 393224 | tf_op jit(solution)/shard_map/ppermute | solution.py:175
  12.8 0.1 collective-permute-start.2
  12.9 2.4 %collective-permute-done.3 = f32[128,256]{1,0:T(8,128)S(1)} collective-permute-done((f32[128,256]{1,0:T(8,128)S(1)}, f32[128,256]{1,0:T(8,128)S(1)}, u32[]{:S(2)}, u32[]{:S(2)}) %collective-permute-start.3) | collective-permute-done | bytes 131104 | tf_op jit(solution)/shard_map/ppermute | solution.py:175
  15.3 3.3 %collective-permute-done.4 = f32[128,256]{1,0:T(8,128)S(1)} collective-permute-done((f32[128,256]{1,0:T(8,128)S(1)}, f32[128,256]{1,0:T(8,128)S(1)}, u32[]{:S(2)}, u32[]{:S(2)}) %collective-permute-start.4) | collective-permute-done | bytes 131104 | tf_op jit(solution)/shard_map/ppermute | solution.py:175
  18.7 0.2 fusion.4
  18.9 0.7 %collective-permute-done.2 = f32[128,256]{1,0:T(8,128)S(1)} collective-permute-done((f32[128,256]{1,0:T(8,128)S(1)}, f32[128,256]{1,0:T(8,128)S(1)}, u32[]{:S(2)}, u32[]{:S(2)}) %collective-permute-start.2) | collective-permute-done | bytes 131104 | tf_op jit(solution)/shard_map/ppermute | solution.py:175
  19.6 0.2 fusion.2
  19.9 0.2 convolution_add_fusion.after
  20.1 2.7 %collective-permute-start.5 = (f32[128,128]{1,0:T(8,128)S(1)}, f32[128,128]{1,0:T(8,128)S(1)}, u32[]{:S(2)}, u32[]{:S(2)}) collective-permute-start(f32[128,128]{1,0:T(8,128)S(1)} %convolution_add_fusion.after), channel_id=1, source_target_pairs={{0,8},{2,10},{4,12},{6,14},{8,0},{10,2},{12,4},{14,6},{1,9},{3,11}... | collective-permute-start | bytes 196616 | tf_op jit(solution)/shard_map/ppermute | solution.py:175
  22.7 0.2 fusion.22
  22.9 0.2 fusion.19
  23.1 0.2 subtract_select_fusion.solved.found
  23.3 0.6 %shard_map.88.written = f32[128,128]{1,0:T(8,128)} custom-call(f32[128,128]{1,0:T(8,128)S(1)} %subtract_select_fusion.solved.found, f32[128,128]{1,0:T(8,128)S(1)} %slice_select_fusion.after.weight), custom_call_target="tpu_custom_call" | custom-call | bytes 65536 | tf_op jit(solution)/shard_map/pallas_call | solution.py:105
  24.0 1.0 %shard_map.87 = bf16[2048,256]{1,0:T(8,128)(2,1)} custom-call(bf16[2048,256]{1,0:T(8,128)(2,1)S(1)} %get-tuple-element.13.solved, f32[128,128]{1,0:T(8,128)S(1)} %convolution_add_fusion.after), custom_call_target="tpu_custom_call" | custom-call | bytes 65536 | tf_op jit(solution)/shard_map/pallas_call | solution.py:105
  25.0 0.3 %collective-permute-done.5.came = f32[128,128]{1,0:T(8,128)S(1)} collective-permute-done((f32[128,128]{1,0:T(8,128)S(1)}, f32[128,128]{1,0:T(8,128)S(1)}, u32[]{:S(2)}, u32[]{:S(2)}) %collective-permute-start.5) | collective-permute-done | bytes 65568 | tf_op jit(solution)/shard_map/ppermute | solution.py:175
  (9 shorter events, 0.1 us)
Async XLA Ops:
  0.6 7.3 %collective-permute-start = (f32[128,128]{1,0:T(8,128)}, f32[128,128]{1,0:T(8,128)S(1)}, u32[]{:S(2)}, u32[]{:S(2)}) collective-permute-start(f32[128,128]{1,0:T(8,128)} %bitcast.12), channel_id=1, source_target_pairs={{2,0},{4,2},{6,4},{8,6},{10,8},{12,10},{14,12},{3,1},{5,3},{7,5},{... | collective-permute-start | bytes 196616 | tf_op jit(solution)/shard_map/ppermute | solution.py:157
  4.3 3.8 %collective-permute-start.1 = (f32[256,128]{1,0:T(8,128)S(1)}, f32[256,128]{1,0:T(8,128)S(1)}, u32[]{:S(2)}, u32[]{:S(2)}) collective-permute-start(f32[256,128]{1,0:T(8,128)S(1)} %get-tuple-element.18), channel_id=1, source_target_pairs={{0,1},{1,0},{2,3},{3,2},{4,5},{5,4},{6,7},{7,6},{8,9},{9,8},{10,11... | collective-permute-start | bytes 393224 | tf_op jit(solution)/shard_map/ppermute | solution.py:162
  8.3 6.9 %collective-permute-start.3 = (f32[128,256]{1,0:T(8,128)S(1)}, f32[128,256]{1,0:T(8,128)S(1)}, u32[]{:S(2)}, u32[]{:S(2)}) collective-permute-start(f32[128,256]{1,0:T(8,128)S(1)} %pad_maximum_fusion.2), channel_id=1, source_target_pairs={{0,4},{2,6},{4,0},{6,2},{8,12},{10,14},{12,8},{14,10},{1,5},{3,7},... | collective-permute-start | bytes 393224 | tf_op jit(solution)/shard_map/ppermute | solution.py:175
  11.0 7.6 %collective-permute-start.4 = (f32[128,256]{1,0:T(8,128)S(1)}, f32[128,256]{1,0:T(8,128)S(1)}, u32[]{:S(2)}, u32[]{:S(2)}) collective-permute-start(f32[128,256]{1,0:T(8,128)S(1)} %pad_maximum_fusion.2), channel_id=1, source_target_pairs={{0,6},{2,4},{4,2},{6,0},{8,14},{10,12},{12,10},{14,8},{1,7},{3,5},... | collective-permute-start | bytes 393224 | tf_op jit(solution)/shard_map/ppermute | solution.py:175
  12.8 6.8 %collective-permute-start.2 = (f32[128,256]{1,0:T(8,128)S(1)}, f32[128,256]{1,0:T(8,128)S(1)}, u32[]{:S(2)}, u32[]{:S(2)}) collective-permute-start(f32[128,256]{1,0:T(8,128)S(1)} %pad_maximum_fusion.2), channel_id=1, source_target_pairs={{0,2},{2,0},{4,6},{6,4},{8,10},{10,8},{12,14},{14,12},{1,3},{3,1},... | collective-permute-start | bytes 393224 | tf_op jit(solution)/shard_map/ppermute | solution.py:175
  20.1 5.2 %collective-permute-start.5 = (f32[128,128]{1,0:T(8,128)S(1)}, f32[128,128]{1,0:T(8,128)S(1)}, u32[]{:S(2)}, u32[]{:S(2)}) collective-permute-start(f32[128,128]{1,0:T(8,128)S(1)} %convolution_add_fusion.after), channel_id=1, source_target_pairs={{0,8},{2,10},{4,12},{6,14},{8,0},{10,2},{12,4},{14,6},{1,9},{3,11}... | collective-permute-start | bytes 196616 | tf_op jit(solution)/shard_map/ppermute | solution.py:175

commit v4 on v3

--- a/solution.py
+++ b/solution.py
@@ -154,7 +154,17 @@
     half = leaf_rhs.shape[1] // 2
     columns = lax.axis_size("pcol")
     column = lax.axis_index("pcol")
-    ahead = lax.ppermute(sep_coupling[0], "pcol", [(i, i - 1) for i in range(1, columns)])
+    own = sep_coupling[0]
+    n = columns
+    ring = [(2, 1), (1, 0), (0, 2), (n - 2, n - 3), (n - 3, n - 1), (n - 1, n - 2)]
+    ring += [(2 * k - a, 2 * k - 1 + a) for k in range(2, n // 2 - 1) for a in (0, 1)]
+    def odd_from():
+        return lax.ppermute(own, "pcol", ring)
+    def even_from():
+        return lax.ppermute(own, "pcol", [(i, i ^ 1) for i in range(n)])
+    o = odd_from()
+    e = even_from()
+    ahead = jnp.where((column & 1) == 0, e, o)
     solved, kept, sent, inverse = leaves(
         parent, leaf_inverse, leaf_rhs, leaf_coupling, sep_rhs, sep_inverse[0]
     )
@@ -176,7 +186,7 @@
 
     late = []
     distance = 1
-    flights = {d: swap(total, d) for d in (1, 2, 3)}
+    flights = dict(zip((3, 2, 1), lax.optimization_barrier([swap(total, d) for d in (3, 2, 1)])))
     while distance < columns:
         last = 2 * distance >= columns
         if distance == 1:

time: 25.5 us -> 25 us (0.980)
  waiting for transfers between devices: 9.84 us -> 8.44 us
  starting transfers between devices: 9.02 us -> 9.99 us
    ppermute x1 -> x2, starting transfers between devices: 1.29 us -> 4.58 us  [the longest x1 3 us: even_from(): return lax.ppermute(own, 'pcol', [(i, i ^ 1) for i in range(n)])]
    ppermute x1 -> x2, waiting for transfers between devices: 3.11 us -> 0.44 us  [the longest x1 0.44 us: odd_from(): return lax.ppermute(own, 'pcol', ring)]
    ppermute x4, starting transfers between devices: 7.21 us -> 5.34 us  [swap(): return lax.ppermute(array, 'pcol', pairs)]
    ppermute x1, waiting for transfers between devices: 0.01 us -> 0.69 us  [on_device(): came = lax.ppermute(sent, 'prow', [(0, 1), (1, 0)])]
    ppermute x4, waiting for transfers between devices: 6.73 us -> 7.31 us  [swap(): return lax.ppermute(array, 'pcol', pairs)]
    ppermute x1, starting transfers between devices: 0.52 us -> 0.07 us  [on_device(): came = lax.ppermute(sent, 'prow', [(0, 1), (1, 0)])]
  transfers between devices with their start and end apart: 6 -> 7, of which waited for: 5 -> 6; matrix products, arithmetic and copies ran while one was open for 4% -> 3% of each run, Pallas kernels for 16% -> 16%
where the time goes in v4:
time: 25 us; the launch traced here: 24.9 us
  starting transfers between devices  9.99 us (40%)
  waiting for transfers between devices  8.44 us (34%)
  Pallas kernels  3.98 us (16%)
  matrix products  1.53 us (6%)
  between operations  0.8 us (3%)
    ppermute x4, waiting for transfers between devices, swap(): return lax.ppermute(array, 'pcol', pairs)  7.31 us
    ppermute x4, starting transfers between devices, swap(): return lax.ppermute(array, 'pcol', pairs)  5.34 us
    ppermute x1, starting transfers between devices, even_from(): return lax.ppermute(own, 'pcol', [(i, i ^ 1) for i in range(n)])  3 us
    pallas_call x1, Pallas kernels, leaves(): pl.pallas_call(leaf_kernel, out_shape=(pltpu.VMEM(rhs.shape, jnp.bfloat16...  2.35 us
    pallas_call x2, Pallas kernels, store(): pl.pallas_call(store_kernel, out_shape=pltpu.HBM(array.shape, array.dtype...  1.62 us
    ppermute x1, starting transfers between devices, odd_from(): return lax.ppermute(own, 'pcol', ring)  1.58 us
    dot_general x8, matrix products, mul(): return jnp.dot(a, b, precision=lax.Precision.HIGH)  1.53 us
    ppermute x1, waiting for transfers between devices, on_device(): came = lax.ppermute(sent, 'prow', [(0, 1), (1, 0)])  0.69 us
  transfers between devices with their start and end apart: 7, of which 6 were waited for; matrix products, arithmetic and copies ran while one was open for 3% of the time, Pallas kernels for 16%

profile of v4, /device:TPU:0, one launch (start us, length us, event | category | flops | bytes accessed | tf_op | source)
XLA Modules:
  0.0 24.9 jit_solution(13965802930729030407)
XLA Ops:
  0.6 3.0 %collective-permute-start = (f32[128,128]{1,0:T(8,128)}, f32[128,128]{1,0:T(8,128)S(1)}, u32[]{:S(2)}, u32[]{:S(2)}) collective-permute-start(f32[128,128]{1,0:T(8,128)} %bitcast.9), channel_id=1, source_target_pairs={{0,2},{2,0},{4,6},{6,4},{8,10},{10,8},{12,14},{14,12},{1,3},{3,1},... | collective-permute-start | bytes 196616 | tf_op jit(solution)/shard_map/ppermute | solution.py:164
  3.6 1.6 %collective-permute-start.1 = (f32[128,128]{1,0:T(8,128)}, f32[128,128]{1,0:T(8,128)S(1)}, u32[]{:S(2)}, u32[]{:S(2)}) collective-permute-start(f32[128,128]{1,0:T(8,128)} %bitcast.10), channel_id=1, source_target_pairs={{4,2},{2,0},{0,4},{12,10},{10,14},{14,12},{8,6},{6,8},{5,3},{3,1},... | collective-permute-start | bytes 196616 | tf_op jit(solution)/shard_map/ppermute | solution.py:162
  5.2 2.4 %shard_map.86 = (bf16[2048,256]{1,0:T(8,128)(2,1)S(1)}, f32[256,128]{1,0:T(8,128)S(1)}, f32[256,128]{1,0:T(8,128)S(1)}, f32[128,128]{1,0:T(8,128)S(1)}) custom-call(s32[16]{0:T(128)} %parent_in.1, bf16[16,128,128]{2,1,0:T(8,128)(2,1)} %inverse_in.1, bf16[2048,256]{1,0:T(8,128)(2,1)} %rhs_in.1, bf16[128,2048]{1,0:T(8,128)(2,1)} %coupling_in.1, ...), custom_call_target="tpu_custom_call" | custom-call | tf_op jit(solution)/shard_map/pallas_call | solution.py:80
  7.6 0.1 collective-permute-start.2
  7.7 0.0 collective-permute-done
  7.7 0.4 %collective-permute-done.1 = f32[128,128]{1,0:T(8,128)S(1)} collective-permute-done((f32[128,128]{1,0:T(8,128)}, f32[128,128]{1,0:T(8,128)S(1)}, u32[]{:S(2)}, u32[]{:S(2)}) %collective-permute-start.1) | collective-permute-done | bytes 65568 | tf_op jit(solution)/shard_map/ppermute | solution.py:162
  8.1 0.2 convolution_negate_fusion.1
  8.3 0.7 %collective-permute-done.2 = f32[256,128]{1,0:T(8,128)S(1)} collective-permute-done((f32[256,128]{1,0:T(8,128)S(1)}, f32[256,128]{1,0:T(8,128)S(1)}, u32[]{:S(2)}, u32[]{:S(2)}) %collective-permute-start.2) | collective-permute-done | bytes 131104 | tf_op jit(solution)/shard_map/ppermute | solution.py:172
  9.0 0.2 convolution_add_fusion.1
  9.2 2.5 %collective-permute-start.3 = (f32[128,256]{1,0:T(8,128)S(1)}, f32[128,256]{1,0:T(8,128)S(1)}, u32[]{:S(2)}, u32[]{:S(2)}) collective-permute-start(f32[128,256]{1,0:T(8,128)S(1)} %pad_maximum_fusion.2), channel_id=1, source_target_pairs={{0,6},{2,4},{4,2},{6,0},{8,14},{10,12},{12,10},{14,8},{1,7},{3,5},... | collective-permute-start | bytes 393224 | tf_op jit(solution)/shard_map/ppermute | solution.py:185
  11.8 0.0 collective-permute-start.4
  11.8 1.0 %collective-permute-start.5 = (f32[128,256]{1,0:T(8,128)S(1)}, f32[128,256]{1,0:T(8,128)S(1)}, u32[]{:S(2)}, u32[]{:S(2)}) collective-permute-start(f32[128,256]{1,0:T(8,128)S(1)} %pad_maximum_fusion.2), channel_id=1, source_target_pairs={{0,2},{2,0},{4,6},{6,4},{8,10},{10,8},{12,14},{14,12},{1,3},{3,1},... | collective-permute-start | bytes 393224 | tf_op jit(solution)/shard_map/ppermute | solution.py:185
  12.8 3.7 %collective-permute-done.3 = f32[128,256]{1,0:T(8,128)S(1)} collective-permute-done((f32[128,256]{1,0:T(8,128)S(1)}, f32[128,256]{1,0:T(8,128)S(1)}, u32[]{:S(2)}, u32[]{:S(2)}) %collective-permute-start.3) | collective-permute-done | bytes 131104 | tf_op jit(solution)/shard_map/ppermute | solution.py:185
  16.5 1.1 %collective-permute-done.4 = f32[128,256]{1,0:T(8,128)S(1)} collective-permute-done((f32[128,256]{1,0:T(8,128)S(1)}, f32[128,256]{1,0:T(8,128)S(1)}, u32[]{:S(2)}, u32[]{:S(2)}) %collective-permute-start.4) | collective-permute-done | bytes 131104 | tf_op jit(solution)/shard_map/ppermute | solution.py:185
  17.7 0.9 %collective-permute-done.5 = f32[128,256]{1,0:T(8,128)S(1)} collective-permute-done((f32[128,256]{1,0:T(8,128)S(1)}, f32[128,256]{1,0:T(8,128)S(1)}, u32[]{:S(2)}, u32[]{:S(2)}) %collective-permute-start.5) | collective-permute-done | bytes 131104 | tf_op jit(solution)/shard_map/ppermute | solution.py:185
  18.6 0.2 fusion.3
  18.8 0.2 fusion.1
  19.1 0.2 convolution_add_fusion.after
  19.3 1.8 %collective-permute-start.6 = (f32[128,128]{1,0:T(8,128)S(1)}, f32[128,128]{1,0:T(8,128)S(1)}, u32[]{:S(2)}, u32[]{:S(2)}) collective-permute-start(f32[128,128]{1,0:T(8,128)S(1)} %convolution_add_fusion.after), channel_id=1, source_target_pairs={{0,8},{2,10},{4,12},{6,14},{8,0},{10,2},{12,4},{14,6},{1,9},{3,11}... | collective-permute-start | bytes 196616 | tf_op jit(solution)/shard_map/ppermute | solution.py:185
  21.0 0.2 fusion.23
  21.2 0.2 fusion.20
  21.5 0.2 subtract_select_fusion.solved.found
  21.7 0.6 %shard_map.88.written = f32[128,128]{1,0:T(8,128)} custom-call(f32[128,128]{1,0:T(8,128)S(1)} %subtract_select_fusion.solved.found, f32[128,128]{1,0:T(8,128)S(1)} %slice_select_fusion.after.weight), custom_call_target="tpu_custom_call" | custom-call | bytes 65536 | tf_op jit(solution)/shard_map/pallas_call | solution.py:105
  22.3 1.0 %shard_map.87 = bf16[2048,256]{1,0:T(8,128)(2,1)} custom-call(bf16[2048,256]{1,0:T(8,128)(2,1)S(1)} %get-tuple-element.16.solved, f32[128,128]{1,0:T(8,128)S(1)} %convolution_add_fusion.after), custom_call_target="tpu_custom_call" | custom-call | bytes 65536 | tf_op jit(solution)/shard_map/pallas_call | solution.py:105
  23.3 1.5 %collective-permute-done.6.came = f32[128,128]{1,0:T(8,128)S(1)} collective-permute-done((f32[128,128]{1,0:T(8,128)S(1)}, f32[128,128]{1,0:T(8,128)S(1)}, u32[]{:S(2)}, u32[]{:S(2)}) %collective-permute-start.6) | collective-permute-done | bytes 65568 | tf_op jit(solution)/shard_map/ppermute | solution.py:185
  (8 shorter events, 0.1 us)
Async XLA Ops:
  0.6 7.0 %collective-permute-start = (f32[128,128]{1,0:T(8,128)}, f32[128,128]{1,0:T(8,128)S(1)}, u32[]{:S(2)}, u32[]{:S(2)}) collective-permute-start(f32[128,128]{1,0:T(8,128)} %bitcast.9), channel_id=1, source_target_pairs={{0,2},{2,0},{4,6},{6,4},{8,10},{10,8},{12,14},{14,12},{1,3},{3,1},... | collective-permute-start | bytes 196616 | tf_op jit(solution)/shard_map/ppermute | solution.py:164
  3.6 4.5 %collective-permute-start.1 = (f32[128,128]{1,0:T(8,128)}, f32[128,128]{1,0:T(8,128)S(1)}, u32[]{:S(2)}, u32[]{:S(2)}) collective-permute-start(f32[128,128]{1,0:T(8,128)} %bitcast.10), channel_id=1, source_target_pairs={{4,2},{2,0},{0,4},{12,10},{10,14},{14,12},{8,6},{6,8},{5,3},{3,1},... | collective-permute-start | bytes 196616 | tf_op jit(solution)/shard_map/ppermute | solution.py:162
  7.6 1.4 %collective-permute-start.2 = (f32[256,128]{1,0:T(8,128)S(1)}, f32[256,128]{1,0:T(8,128)S(1)}, u32[]{:S(2)}, u32[]{:S(2)}) collective-permute-start(f32[256,128]{1,0:T(8,128)S(1)} %get-tuple-element.21), channel_id=1, source_target_pairs={{0,1},{1,0},{2,3},{3,2},{4,5},{5,4},{6,7},{7,6},{8,9},{9,8},{10,11... | collective-permute-start | bytes 393224 | tf_op jit(solution)/shard_map/ppermute | solution.py:172
  9.2 7.3 %collective-permute-start.3 = (f32[128,256]{1,0:T(8,128)S(1)}, f32[128,256]{1,0:T(8,128)S(1)}, u32[]{:S(2)}, u32[]{:S(2)}) collective-permute-start(f32[128,256]{1,0:T(8,128)S(1)} %pad_maximum_fusion.2), channel_id=1, source_target_pairs={{0,6},{2,4},{4,2},{6,0},{8,14},{10,12},{12,10},{14,8},{1,7},{3,5},... | collective-permute-start | bytes 393224 | tf_op jit(solution)/shard_map/ppermute | solution.py:185
  11.8 5.9 %collective-permute-start.4 = (f32[128,256]{1,0:T(8,128)S(1)}, f32[128,256]{1,0:T(8,128)S(1)}, u32[]{:S(2)}, u32[]{:S(2)}) collective-permute-start(f32[128,256]{1,0:T(8,128)S(1)} %pad_maximum_fusion.2), channel_id=1, source_target_pairs={{0,4},{2,6},{4,0},{6,2},{8,12},{10,14},{12,8},{14,10},{1,5},{3,7},... | collective-permute-start | bytes 393224 | tf_op jit(solution)/shard_map/ppermute | solution.py:185
  11.8 6.8 %collective-permute-start.5 = (f32[128,256]{1,0:T(8,128)S(1)}, f32[128,256]{1,0:T(8,128)S(1)}, u32[]{:S(2)}, u32[]{:S(2)}) collective-permute-start(f32[128,256]{1,0:T(8,128)S(1)} %pad_maximum_fusion.2), channel_id=1, source_target_pairs={{0,2},{2,0},{4,6},{6,4},{8,10},{10,8},{12,14},{14,12},{1,3},{3,1},... | collective-permute-start | bytes 393224 | tf_op jit(solution)/shard_map/ppermute | solution.py:185
  19.3 5.6 %collective-permute-start.6 = (f32[128,128]{1,0:T(8,128)S(1)}, f32[128,128]{1,0:T(8,128)S(1)}, u32[]{:S(2)}, u32[]{:S(2)}) collective-permute-start(f32[128,128]{1,0:T(8,128)S(1)} %convolution_add_fusion.after), channel_id=1, source_target_pairs={{0,8},{2,10},{4,12},{6,14},{8,0},{10,2},{12,4},{14,6},{1,9},{3,11}... | collective-permute-start | bytes 196616 | tf_op jit(solution)/shard_map/ppermute | solution.py:185

commit v5 on v4

--- a/solution.py
+++ b/solution.py
@@ -125,6 +125,34 @@
     return dot(ah, bh) + (dot(ah, bl) + dot(al, bh))
 
 
+def top_kernel(own, near, across, far, out):
+    column = lax.axis_index("pcol")
+    odd = (column & 1) != 0
+    high = (column & 2) != 0
+    half = out.shape[1]
+    low_own, high_own = jnp.where(odd, near[...], own[...]), jnp.where(odd, own[...], near[...])
+    low_other = jnp.where(odd, far[...], across[...])
+    high_other = jnp.where(odd, across[...], far[...])
+    first = jnp.where(high, low_other, low_own)
+    second = jnp.where(high, high_other, high_own)
+    third = jnp.where(high, low_own, low_other)
+    fourth = jnp.where(high, high_own, high_other)
+    lower = second[:, :half] + product(second[:, half:], first[:, :half])
+    upper = product(fourth[:, half:], third)
+    out[...] = fourth[:, :half] + upper[:, :half] + product(upper[:, half:], lower)
+
+
+def top(own, near, across, far):
+    block, width = own.shape
+    return pl.pallas_call(
+        top_kernel,
+        out_shape=pltpu.VMEM((block, width // 2), own.dtype),
+        in_specs=[VMEM] * 4,
+        out_specs=VMEM,
+        cost_estimate=pl.CostEstimate(flops=0, bytes_accessed=2**16, transcendentals=0),
+    )(*[pltpu.with_memory_space_constraint(a, pltpu.VMEM) for a in (own, near, across, far)])
+
+
 def finish_kernel(distance, found, weight, came, written, out, result, sem):
     del written
 
@@ -184,34 +212,42 @@
         pairs = [(i, i ^ distance) for i in range(columns) if i ^ distance < columns]
         return lax.ppermute(array, "pcol", pairs)
 
-    late = []
-    distance = 1
-    flights = dict(zip((3, 2, 1), lax.optimization_barrier([swap(total, d) for d in (3, 2, 1)])))
-    while distance < columns:
-        last = 2 * distance >= columns
-        if distance == 1:
-            came = flights[1]
-        elif distance == 2:
-            odd = (column & 1) != 0
-            came = join(
-                jnp.where(odd, flights[3], flights[2]), jnp.where(odd, flights[2], flights[3])
-            )
-        else:
-            total = total[:, :half] if last else total
-            came = swap(total, distance)
-        if last:
-            late, total_after = lax.optimization_barrier((late, total))
-            for above, block_came in late:
-                moved = mul(weight, block_came)
-                found = jnp.where(above, found - moved[:, :half], found)
-                weight = jnp.where(above, moved[:, half:], weight)
-            solved = store(solved, total_after)
-            found = finish(distance, found, weight, came)
-            break
+    flights = {}
+    order = (2, 1, 3)
+    arrived = lax.optimization_barrier([swap(total, d) for d in order])
+    flights = dict(zip(order, arrived))
+    odd = (column & 1) != 0
+
+    def other_pair(pieces):
+        return join(jnp.where(odd, pieces[3], pieces[2]), jnp.where(odd, pieces[2], pieces[3]))
+
+    if columns == 8:
+        total = top(total, flights[1], flights[2], flights[3])
+        late = ()
+    else:
+        late = ((1, flights[1]), (2, other_pair(flights)))
+        for distance, came in late:
+            upper = (column & distance) != 0
+            total = join(jnp.where(upper, came, total), jnp.where(upper, total, came))
+    distance = 4
+    while 2 * distance < columns:
+        came = swap(total, distance)
         upper = (column & distance) != 0
-        late.append((upper, came))
+        late += ((distance, came),)
         total = join(jnp.where(upper, came, total), jnp.where(upper, total, came))
         distance *= 2
+    total = total[:, :half]
+    came = swap(total, distance)
+    flights, late, total = lax.optimization_barrier((flights, late, total))
+    if columns == 8:
+        late = ((1, flights[1]), (2, other_pair(flights)))
+    for place, block_came in late:
+        above = (column & place) != 0
+        moved = mul(weight, block_came)
+        found = jnp.where(above, found - moved[:, :half], found)
+        weight = jnp.where(above, moved[:, half:], weight)
+    solved = store(solved, total)
+    found = finish(distance, found, weight, came)
     return solved, found
 def solution(mesh):
     return jax.shard_map(

time: 25 us -> 24.5 us (0.980)
  waiting for transfers between devices: 8.44 us -> 7.77 us
  Pallas kernels: 3.98 us -> 4.42 us
  matrix products: 1.53 us -> 1.14 us
    ppermute x4, waiting for transfers between devices: 7.31 us -> 6.63 us  [swap(): return lax.ppermute(array, 'pcol', pairs)]
    pallas_call x0 -> x1, Pallas kernels: none -> 0.43 us  [top(): pl.pallas_call(top_kernel, out_shape=pltpu.VMEM((block, width // 2), own....]
    dot_general x8 -> x6, matrix products: 1.53 us -> 1.14 us  [mul(): return jnp.dot(a, b, precision=lax.Precision.HIGH)]
  transfers between devices with their start and end apart: 7 -> 7, of which waited for: 6 -> 5; matrix products, arithmetic and copies ran while one was open for 3% -> 4% of each run, Pallas kernels for 16% -> 16%
where the time goes in v5:
time: 24.5 us; the launch traced here: 24.3 us
  starting transfers between devices  10.2 us (42%)
  waiting for transfers between devices  7.77 us (32%)
  Pallas kernels  4.42 us (18%)
  matrix products  1.14 us (5%)
  between operations  0.77 us (3%)
    ppermute x4, waiting for transfers between devices, swap(): return lax.ppermute(array, 'pcol', pairs)  6.63 us
    ppermute x4, starting transfers between devices, swap(): return lax.ppermute(array, 'pcol', pairs)  5.51 us
    ppermute x1, starting transfers between devices, even_from(): return lax.ppermute(own, 'pcol', [(i, i ^ 1) for i in range(n)])  3 us
    pallas_call x1, Pallas kernels, leaves(): pl.pallas_call(leaf_kernel, out_shape=(pltpu.VMEM(rhs.shape, jnp.bfloat16...  2.35 us
    pallas_call x2, Pallas kernels, store(): pl.pallas_call(store_kernel, out_shape=pltpu.HBM(array.shape, array.dtype...  1.62 us
    ppermute x1, starting transfers between devices, odd_from(): return lax.ppermute(own, 'pcol', ring)  1.58 us
    dot_general x6, matrix products, mul(): return jnp.dot(a, b, precision=lax.Precision.HIGH)  1.14 us
    ppermute x1, waiting for transfers between devices, on_device(): came = lax.ppermute(sent, 'prow', [(0, 1), (1, 0)])  0.69 us
  transfers between devices with their start and end apart: 7, of which 5 were waited for; matrix products, arithmetic and copies ran while one was open for 4% of the time, Pallas kernels for 16%

profile of v5, /device:TPU:0, one launch (start us, length us, event | category | flops | bytes accessed | tf_op | source)
XLA Modules:
  0.0 24.3 jit_solution(9817332684781387756)
XLA Ops:
  0.6 3.0 %collective-permute-start = (f32[128,128]{1,0:T(8,128)}, f32[128,128]{1,0:T(8,128)S(1)}, u32[]{:S(2)}, u32[]{:S(2)}) collective-permute-start(f32[128,128]{1,0:T(8,128)} %bitcast.8), channel_id=1, source_target_pairs={{0,2},{2,0},{4,6},{6,4},{8,10},{10,8},{12,14},{14,12},{1,3},{3,1},... | collective-permute-start | bytes 196616 | tf_op jit(solution)/shard_map/ppermute | solution.py:192
  3.6 1.6 %collective-permute-start.1 = (f32[128,128]{1,0:T(8,128)}, f32[128,128]{1,0:T(8,128)S(1)}, u32[]{:S(2)}, u32[]{:S(2)}) collective-permute-start(f32[128,128]{1,0:T(8,128)} %bitcast.9), channel_id=1, source_target_pairs={{4,2},{2,0},{0,4},{12,10},{10,14},{14,12},{8,6},{6,8},{5,3},{3,1},... | collective-permute-start | bytes 196616 | tf_op jit(solution)/shard_map/ppermute | solution.py:190
  5.2 2.4 %shard_map.86 = (bf16[2048,256]{1,0:T(8,128)(2,1)S(1)}, f32[256,128]{1,0:T(8,128)S(1)}, f32[256,128]{1,0:T(8,128)S(1)}, f32[128,128]{1,0:T(8,128)S(1)}) custom-call(s32[16]{0:T(128)} %parent_in.1, bf16[16,128,128]{2,1,0:T(8,128)(2,1)} %inverse_in.1, bf16[2048,256]{1,0:T(8,128)(2,1)} %rhs_in.1, bf16[128,2048]{1,0:T(8,128)(2,1)} %coupling_in.1, ...), custom_call_target="tpu_custom_call" | custom-call | tf_op jit(solution)/shard_map/pallas_call | solution.py:80
  7.6 0.1 collective-permute-start.2
  7.7 0.0 collective-permute-done
  7.7 0.4 %collective-permute-done.1 = f32[128,128]{1,0:T(8,128)S(1)} collective-permute-done((f32[128,128]{1,0:T(8,128)}, f32[128,128]{1,0:T(8,128)S(1)}, u32[]{:S(2)}, u32[]{:S(2)}) %collective-permute-start.1) | collective-permute-done | bytes 65568 | tf_op jit(solution)/shard_map/ppermute | solution.py:190
  8.1 0.2 convolution_negate_fusion.1
  8.3 0.7 %collective-permute-done.2 = f32[256,128]{1,0:T(8,128)S(1)} collective-permute-done((f32[256,128]{1,0:T(8,128)S(1)}, f32[256,128]{1,0:T(8,128)S(1)}, u32[]{:S(2)}, u32[]{:S(2)}) %collective-permute-start.2) | collective-permute-done | bytes 131104 | tf_op jit(solution)/shard_map/ppermute | solution.py:200
  9.0 0.2 convolution_add_fusion
  9.2 1.0 %collective-permute-start.3 = (f32[128,256]{1,0:T(8,128)S(1)}, f32[128,256]{1,0:T(8,128)S(1)}, u32[]{:S(2)}, u32[]{:S(2)}) collective-permute-start(f32[128,256]{1,0:T(8,128)S(1)} %pad_maximum_fusion.own), channel_id=1, source_target_pairs={{0,4},{2,6},{4,0},{6,2},{8,12},{10,14},{12,8},{14,10},{1,5},{3,7},... | collective-permute-start | bytes 393224 | tf_op jit(solution)/shard_map/ppermute | solution.py:213
  10.2 2.1 %collective-permute-start.4 = (f32[128,256]{1,0:T(8,128)S(1)}, f32[128,256]{1,0:T(8,128)S(1)}, u32[]{:S(2)}, u32[]{:S(2)}) collective-permute-start(f32[128,256]{1,0:T(8,128)S(1)} %pad_maximum_fusion.own), channel_id=1, source_target_pairs={{0,2},{2,0},{4,6},{6,4},{8,10},{10,8},{12,14},{14,12},{1,3},{3,1},... | collective-permute-start | bytes 393224 | tf_op jit(solution)/shard_map/ppermute | solution.py:213
  12.3 0.4 %collective-permute-start.5 = (f32[128,256]{1,0:T(8,128)S(1)}, f32[128,256]{1,0:T(8,128)S(1)}, u32[]{:S(2)}, u32[]{:S(2)}) collective-permute-start(f32[128,256]{1,0:T(8,128)S(1)} %pad_maximum_fusion.own), channel_id=1, source_target_pairs={{0,6},{2,4},{4,2},{6,0},{8,14},{10,12},{12,10},{14,8},{1,7},{3,5},... | collective-permute-start | bytes 393224 | tf_op jit(solution)/shard_map/ppermute | solution.py:213
  12.8 2.6 %collective-permute-done.3.across = f32[128,256]{1,0:T(8,128)S(1)} collective-permute-done((f32[128,256]{1,0:T(8,128)S(1)}, f32[128,256]{1,0:T(8,128)S(1)}, u32[]{:S(2)}, u32[]{:S(2)}) %collective-permute-start.3) | collective-permute-done | bytes 131104 | tf_op jit(solution)/shard_map/ppermute | solution.py:213
  15.4 3.3 %collective-permute-done.4.near = f32[128,256]{1,0:T(8,128)S(1)} collective-permute-done((f32[128,256]{1,0:T(8,128)S(1)}, f32[128,256]{1,0:T(8,128)S(1)}, u32[]{:S(2)}, u32[]{:S(2)}) %collective-permute-start.4) | collective-permute-done | bytes 131104 | tf_op jit(solution)/shard_map/ppermute | solution.py:213
  18.7 0.0 collective-permute-done.5.far
  18.7 0.4 %shard_map.87.after = f32[128,128]{1,0:T(8,128)S(1)} custom-call(f32[128,256]{1,0:T(8,128)S(1)} %pad_maximum_fusion.own, f32[128,256]{1,0:T(8,128)S(1)} %collective-permute-done.4.near, f32[128,256]{1,0:T(8,128)S(1)} %collective-permute-done.3.across, f32[128,256]{1,0:T(8,128)S(1)} %collective-permute-done.5.far), custom_call_target="tpu_custom_call" | custom-call | bytes 65536 | tf_op jit(solution)/shard_map/pallas_call | solution.py:147
  19.1 2.0 %collective-permute-start.6 = (f32[128,128]{1,0:T(8,128)S(1)}, f32[128,128]{1,0:T(8,128)S(1)}, u32[]{:S(2)}, u32[]{:S(2)}) collective-permute-start(f32[128,128]{1,0:T(8,128)S(1)} %shard_map.87.after), channel_id=1, source_target_pairs={{0,8},{2,10},{4,12},{6,14},{8,0},{10,2},{12,4},{14,6},{1,9},{3,11}... | collective-permute-start | bytes 196616 | tf_op jit(solution)/shard_map/ppermute | solution.py:213
  21.1 0.2 fusion.13
  21.3 0.2 fusion.4
  21.5 0.2 fusion
  21.7 0.2 subtract_select_fusion.solved.found
  21.9 0.6 %shard_map.89.written = f32[128,128]{1,0:T(8,128)} custom-call(f32[128,128]{1,0:T(8,128)S(1)} %subtract_select_fusion.solved.found, f32[128,128]{1,0:T(8,128)S(1)} %slice_select_fusion.after.weight), custom_call_target="tpu_custom_call" | custom-call | bytes 65536 | tf_op jit(solution)/shard_map/pallas_call | solution.py:105
  22.6 1.0 %shard_map.88 = bf16[2048,256]{1,0:T(8,128)(2,1)} custom-call(bf16[2048,256]{1,0:T(8,128)(2,1)S(1)} %get-tuple-element.15.solved, f32[128,128]{1,0:T(8,128)S(1)} %shard_map.87.after), custom_call_target="tpu_custom_call" | custom-call | bytes 65536 | tf_op jit(solution)/shard_map/pallas_call | solution.py:105
  23.6 0.7 %collective-permute-done.6.came = f32[128,128]{1,0:T(8,128)S(1)} collective-permute-done((f32[128,128]{1,0:T(8,128)S(1)}, f32[128,128]{1,0:T(8,128)S(1)}, u32[]{:S(2)}, u32[]{:S(2)}) %collective-permute-start.6) | collective-permute-done | bytes 65568 | tf_op jit(solution)/shard_map/ppermute | solution.py:213
  (6 shorter events, 0.1 us)
Async XLA Ops:
  0.6 7.0 %collective-permute-start = (f32[128,128]{1,0:T(8,128)}, f32[128,128]{1,0:T(8,128)S(1)}, u32[]{:S(2)}, u32[]{:S(2)}) collective-permute-start(f32[128,128]{1,0:T(8,128)} %bitcast.8), channel_id=1, source_target_pairs={{0,2},{2,0},{4,6},{6,4},{8,10},{10,8},{12,14},{14,12},{1,3},{3,1},... | collective-permute-start | bytes 196616 | tf_op jit(solution)/shard_map/ppermute | solution.py:192
  3.6 4.5 %collective-permute-start.1 = (f32[128,128]{1,0:T(8,128)}, f32[128,128]{1,0:T(8,128)S(1)}, u32[]{:S(2)}, u32[]{:S(2)}) collective-permute-start(f32[128,128]{1,0:T(8,128)} %bitcast.9), channel_id=1, source_target_pairs={{4,2},{2,0},{0,4},{12,10},{10,14},{14,12},{8,6},{6,8},{5,3},{3,1},... | collective-permute-start | bytes 196616 | tf_op jit(solution)/shard_map/ppermute | solution.py:190
  7.6 1.4 %collective-permute-start.2 = (f32[256,128]{1,0:T(8,128)S(1)}, f32[256,128]{1,0:T(8,128)S(1)}, u32[]{:S(2)}, u32[]{:S(2)}) collective-permute-start(f32[256,128]{1,0:T(8,128)S(1)} %get-tuple-element.20), channel_id=1, source_target_pairs={{0,1},{1,0},{2,3},{3,2},{4,5},{5,4},{6,7},{7,6},{8,9},{9,8},{10,11... | collective-permute-start | bytes 393224 | tf_op jit(solution)/shard_map/ppermute | solution.py:200
  9.2 6.2 %collective-permute-start.3 = (f32[128,256]{1,0:T(8,128)S(1)}, f32[128,256]{1,0:T(8,128)S(1)}, u32[]{:S(2)}, u32[]{:S(2)}) collective-permute-start(f32[128,256]{1,0:T(8,128)S(1)} %pad_maximum_fusion.own), channel_id=1, source_target_pairs={{0,4},{2,6},{4,0},{6,2},{8,12},{10,14},{12,8},{14,10},{1,5},{3,7},... | collective-permute-start | bytes 393224 | tf_op jit(solution)/shard_map/ppermute | solution.py:213
  10.2 8.5 %collective-permute-start.4 = (f32[128,256]{1,0:T(8,128)S(1)}, f32[128,256]{1,0:T(8,128)S(1)}, u32[]{:S(2)}, u32[]{:S(2)}) collective-permute-start(f32[128,256]{1,0:T(8,128)S(1)} %pad_maximum_fusion.own), channel_id=1, source_target_pairs={{0,2},{2,0},{4,6},{6,4},{8,10},{10,8},{12,14},{14,12},{1,3},{3,1},... | collective-permute-start | bytes 393224 | tf_op jit(solution)/shard_map/ppermute | solution.py:213
  12.3 6.3 %collective-permute-start.5 = (f32[128,256]{1,0:T(8,128)S(1)}, f32[128,256]{1,0:T(8,128)S(1)}, u32[]{:S(2)}, u32[]{:S(2)}) collective-permute-start(f32[128,256]{1,0:T(8,128)S(1)} %pad_maximum_fusion.own), channel_id=1, source_target_pairs={{0,6},{2,4},{4,2},{6,0},{8,14},{10,12},{12,10},{14,8},{1,7},{3,5},... | collective-permute-start | bytes 393224 | tf_op jit(solution)/shard_map/ppermute | solution.py:213
  19.1 5.2 %collective-permute-start.6 = (f32[128,128]{1,0:T(8,128)S(1)}, f32[128,128]{1,0:T(8,128)S(1)}, u32[]{:S(2)}, u32[]{:S(2)}) collective-permute-start(f32[128,128]{1,0:T(8,128)S(1)} %shard_map.87.after), channel_id=1, source_target_pairs={{0,8},{2,10},{4,12},{6,14},{8,0},{10,2},{12,4},{14,6},{1,9},{3,11}... | collective-permute-start | bytes 196616 | tf_op jit(solution)/shard_map/ppermute | solution.py:213

commit v6 on v5

--- a/solution.py
+++ b/solution.py
@@ -182,23 +182,20 @@
     half = leaf_rhs.shape[1] // 2
     columns = lax.axis_size("pcol")
     column = lax.axis_index("pcol")
-    own = sep_coupling[0]
     n = columns
+    row = lax.axis_index("prow")
     ring = [(2, 1), (1, 0), (0, 2), (n - 2, n - 3), (n - 3, n - 1), (n - 1, n - 2)]
     ring += [(2 * k - a, 2 * k - 1 + a) for k in range(2, n // 2 - 1) for a in (0, 1)]
-    def odd_from():
-        return lax.ppermute(own, "pcol", ring)
-    def even_from():
-        return lax.ppermute(own, "pcol", [(i, i ^ 1) for i in range(n)])
-    o = odd_from()
-    e = even_from()
-    ahead = jnp.where((column & 1) == 0, e, o)
+    shift = [(2 * i, 2 * (i ^ 1)) for i in range(n)] + [(2 * i + 1, 2 * j + 1) for i, j in ring]
+    ahead = lax.ppermute(sep_coupling[0], ("pcol", "prow"), shift)
     solved, kept, sent, inverse = leaves(
         parent, leaf_inverse, leaf_rhs, leaf_coupling, sep_rhs, sep_inverse[0]
     )
+    came = lax.ppermute(sent, "prow", [(0, 1), (1, 0)])
     b = -mul(ahead, inverse)
-    came = lax.ppermute(sent, "prow", [(0, 1), (1, 0)])
-    b, kept = lax.optimization_barrier((b, kept))
+    b, came = lax.optimization_barrier((b, came))
+    other_b = lax.ppermute(b, "prow", [(0, 1), (1, 0)])
+    b = jnp.where((column & 1) == row, b, other_b)
     sums = kept + came
     minus, onward = sums[:block], sums[block:]
     weight = inverse
@@ -213,7 +210,7 @@
         return lax.ppermute(array, "pcol", pairs)
 
     flights = {}
-    order = (2, 1, 3)
+    order = (1, 2, 3)
     arrived = lax.optimization_barrier([swap(total, d) for d in order])
     flights = dict(zip(order, arrived))
     odd = (column & 1) != 0

time: 24.5 us -> 24.3 us (level)
  starting transfers between devices: 10.2 us -> 9.41 us
  waiting for transfers between devices: 7.77 us -> 8.35 us
    ppermute x2, starting transfers between devices: 4.58 us -> 3.14 us  [the longest x1 2.99 us: on_device(): ahead = lax.ppermute(sep_coupling[0], ('pcol', 'prow'), shift)]
    ppermute x2, waiting for transfers between devices: 0.44 us -> 1.21 us  [the longest x1 1.09 us: on_device(): other_b = lax.ppermute(b, 'prow', [(0, 1), (1, 0)])]
    ppermute x4, starting transfers between devices: 5.51 us -> 6.21 us  [swap(): return lax.ppermute(array, 'pcol', pairs)]
    ppermute x4, waiting for transfers between devices: 6.63 us -> 6.11 us  [swap(): return lax.ppermute(array, 'pcol', pairs)]
    ppermute x1, waiting for transfers between devices: 0.69 us -> 1.02 us  [on_device(): came = lax.ppermute(sent, 'prow', [(0, 1), (1, 0)])]
  transfers between devices with their start and end apart: 7 -> 7, of which waited for: 5 -> 6; matrix products, arithmetic and copies ran while one was open for 4% -> 4% of each run, Pallas kernels for 16% -> 16%
where the time goes in v6:
time: 24.3 us; the launch traced here: 24.2 us
  starting transfers between devices  9.41 us (39%)
  waiting for transfers between devices  8.35 us (34%)
  Pallas kernels  4.41 us (18%)
  matrix products  1.14 us (5%)
  between operations  0.76 us (3%)
    ppermute x4, starting transfers between devices, swap(): return lax.ppermute(array, 'pcol', pairs)  6.21 us
    ppermute x4, waiting for transfers between devices, swap(): return lax.ppermute(array, 'pcol', pairs)  6.11 us
    ppermute x1, starting transfers between devices, on_device(): ahead = lax.ppermute(sep_coupling[0], ('pcol', 'prow'), shift)  2.99 us
    pallas_call x1, Pallas kernels, leaves(): pl.pallas_call(leaf_kernel, out_shape=(pltpu.VMEM(rhs.shape, jnp.bfloat16...  2.35 us
    pallas_call x2, Pallas kernels, store(): pl.pallas_call(store_kernel, out_shape=pltpu.HBM(array.shape, array.dtype...  1.62 us
    dot_general x6, matrix products, mul(): return jnp.dot(a, b, precision=lax.Precision.HIGH)  1.14 us
    ppermute x1, waiting for transfers between devices, on_device(): other_b = lax.ppermute(b, 'prow', [(0, 1), (1, 0)])  1.09 us
    ppermute x1, waiting for transfers between devices, on_device(): came = lax.ppermute(sent, 'prow', [(0, 1), (1, 0)])  1.02 us
  transfers between devices with their start and end apart: 7, of which 6 were waited for; matrix products, arithmetic and copies ran while one was open for 4% of the time, Pallas kernels for 16%

profile of v6, /device:TPU:0, one launch (start us, length us, event | category | flops | bytes accessed | tf_op | source)
XLA Modules:
  0.0 24.2 jit_solution(1284422792620933368)
XLA Ops:
  0.6 3.0 %collective-permute-start = (f32[128,128]{1,0:T(8,128)}, f32[128,128]{1,0:T(8,128)S(1)}, u32[]{:S(2)}, u32[]{:S(2)}) collective-permute-start(f32[128,128]{1,0:T(8,128)} %bitcast.11), channel_id=1, source_target_pairs={{0,2},{2,0},{4,6},{6,4},{8,10},{10,8},{12,14},{14,12},{5,3},{3,1},... | collective-permute-start | bytes 196616 | tf_op jit(solution)/shard_map/ppermute | solution.py:190
  3.6 2.4 %shard_map.86 = (bf16[2048,256]{1,0:T(8,128)(2,1)S(1)}, f32[256,128]{1,0:T(8,128)S(1)}, f32[256,128]{1,0:T(8,128)S(1)}, f32[128,128]{1,0:T(8,128)S(1)}) custom-call(s32[16]{0:T(128)} %parent_in.1, bf16[16,128,128]{2,1,0:T(8,128)(2,1)} %inverse_in.1, bf16[2048,256]{1,0:T(8,128)(2,1)} %rhs_in.1, bf16[128,2048]{1,0:T(8,128)(2,1)} %coupling_in.1, ...), custom_call_target="tpu_custom_call" | custom-call | tf_op jit(solution)/shard_map/pallas_call | solution.py:80
  6.0 0.1 collective-permute-start.1
  6.1 0.1 collective-permute-done
  6.2 0.2 fusion
  6.4 1.0 %collective-permute-done.1 = f32[256,128]{1,0:T(8,128)S(1)} collective-permute-done((f32[256,128]{1,0:T(8,128)S(1)}, f32[256,128]{1,0:T(8,128)S(1)}, u32[]{:S(2)}, u32[]{:S(2)}) %collective-permute-start.1) | collective-permute-done | bytes 131104 | tf_op jit(solution)/shard_map/ppermute | solution.py:194
  7.4 0.1 collective-permute-start.2
  7.6 1.1 %collective-permute-done.2 = f32[128,128]{1,0:T(8,128)S(1)} collective-permute-done((f32[128,128]{1,0:T(8,128)S(1)}, f32[128,128]{1,0:T(8,128)S(1)}, u32[]{:S(2)}, u32[]{:S(2)}) %collective-permute-start.2) | collective-permute-done | bytes 65568 | tf_op jit(solution)/shard_map/ppermute | solution.py:197
  8.7 0.2 convolution_add_fusion
  8.9 1.5 %collective-permute-start.3 = (f32[128,256]{1,0:T(8,128)S(1)}, f32[128,256]{1,0:T(8,128)S(1)}, u32[]{:S(2)}, u32[]{:S(2)}) collective-permute-start(f32[128,256]{1,0:T(8,128)S(1)} %pad_maximum_fusion.own), channel_id=1, source_target_pairs={{0,2},{2,0},{4,6},{6,4},{8,10},{10,8},{12,14},{14,12},{1,3},{3,1},... | collective-permute-start | bytes 393224 | tf_op jit(solution)/shard_map/ppermute | solution.py:210
  10.4 1.6 %collective-permute-start.4 = (f32[128,256]{1,0:T(8,128)S(1)}, f32[128,256]{1,0:T(8,128)S(1)}, u32[]{:S(2)}, u32[]{:S(2)}) collective-permute-start(f32[128,256]{1,0:T(8,128)S(1)} %pad_maximum_fusion.own), channel_id=1, source_target_pairs={{0,4},{2,6},{4,0},{6,2},{8,12},{10,14},{12,8},{14,10},{1,5},{3,7},... | collective-permute-start | bytes 393224 | tf_op jit(solution)/shard_map/ppermute | solution.py:210
  11.9 0.5 %collective-permute-start.5 = (f32[128,256]{1,0:T(8,128)S(1)}, f32[128,256]{1,0:T(8,128)S(1)}, u32[]{:S(2)}, u32[]{:S(2)}) collective-permute-start(f32[128,256]{1,0:T(8,128)S(1)} %pad_maximum_fusion.own), channel_id=1, source_target_pairs={{0,6},{2,4},{4,2},{6,0},{8,14},{10,12},{12,10},{14,8},{1,7},{3,5},... | collective-permute-start | bytes 393224 | tf_op jit(solution)/shard_map/ppermute | solution.py:210
  12.4 2.1 %collective-permute-done.3.near = f32[128,256]{1,0:T(8,128)S(1)} collective-permute-done((f32[128,256]{1,0:T(8,128)S(1)}, f32[128,256]{1,0:T(8,128)S(1)}, u32[]{:S(2)}, u32[]{:S(2)}) %collective-permute-start.3) | collective-permute-done | bytes 131104 | tf_op jit(solution)/shard_map/ppermute | solution.py:210
  14.5 2.3 %collective-permute-done.4.across = f32[128,256]{1,0:T(8,128)S(1)} collective-permute-done((f32[128,256]{1,0:T(8,128)S(1)}, f32[128,256]{1,0:T(8,128)S(1)}, u32[]{:S(2)}, u32[]{:S(2)}) %collective-permute-start.4) | collective-permute-done | bytes 131104 | tf_op jit(solution)/shard_map/ppermute | solution.py:210
  16.7 1.7 %collective-permute-done.5.far = f32[128,256]{1,0:T(8,128)S(1)} collective-permute-done((f32[128,256]{1,0:T(8,128)S(1)}, f32[128,256]{1,0:T(8,128)S(1)}, u32[]{:S(2)}, u32[]{:S(2)}) %collective-permute-start.5) | collective-permute-done | bytes 131104 | tf_op jit(solution)/shard_map/ppermute | solution.py:210
  18.5 0.4 %shard_map.87.after = f32[128,128]{1,0:T(8,128)S(1)} custom-call(f32[128,256]{1,0:T(8,128)S(1)} %pad_maximum_fusion.own, f32[128,256]{1,0:T(8,128)S(1)} %collective-permute-done.3.near, f32[128,256]{1,0:T(8,128)S(1)} %collective-permute-done.4.across, f32[128,256]{1,0:T(8,128)S(1)} %collective-permute-done.5.far), custom_call_target="tpu_custom_call" | custom-call | bytes 65536 | tf_op jit(solution)/shard_map/pallas_call | solution.py:147
  18.9 2.7 %collective-permute-start.6 = (f32[128,128]{1,0:T(8,128)S(1)}, f32[128,128]{1,0:T(8,128)S(1)}, u32[]{:S(2)}, u32[]{:S(2)}) collective-permute-start(f32[128,128]{1,0:T(8,128)S(1)} %shard_map.87.after), channel_id=1, source_target_pairs={{0,8},{2,10},{4,12},{6,14},{8,0},{10,2},{12,4},{14,6},{1,9},{3,11}... | collective-permute-start | bytes 196616 | tf_op jit(solution)/shard_map/ppermute | solution.py:210
  21.6 0.2 fusion.12
  21.8 0.2 fusion.5
  22.0 0.2 fusion.1
  22.3 0.2 subtract_select_fusion.solved.found
  22.5 0.6 %shard_map.89.written = f32[128,128]{1,0:T(8,128)} custom-call(f32[128,128]{1,0:T(8,128)S(1)} %subtract_select_fusion.solved.found, f32[128,128]{1,0:T(8,128)S(1)} %slice_select_fusion.after.weight), custom_call_target="tpu_custom_call" | custom-call | bytes 65536 | tf_op jit(solution)/shard_map/pallas_call | solution.py:105
  23.1 1.0 %shard_map.88 = bf16[2048,256]{1,0:T(8,128)(2,1)} custom-call(bf16[2048,256]{1,0:T(8,128)(2,1)S(1)} %get-tuple-element.15.solved, f32[128,128]{1,0:T(8,128)S(1)} %shard_map.87.after), custom_call_target="tpu_custom_call" | custom-call | bytes 65536 | tf_op jit(solution)/shard_map/pallas_call | solution.py:105
  24.1 0.0 collective-permute-done.6.came
  (7 shorter events, 0.1 us)
Async XLA Ops:
  0.6 5.6 %collective-permute-start = (f32[128,128]{1,0:T(8,128)}, f32[128,128]{1,0:T(8,128)S(1)}, u32[]{:S(2)}, u32[]{:S(2)}) collective-permute-start(f32[128,128]{1,0:T(8,128)} %bitcast.11), channel_id=1, source_target_pairs={{0,2},{2,0},{4,6},{6,4},{8,10},{10,8},{12,14},{14,12},{5,3},{3,1},... | collective-permute-start | bytes 196616 | tf_op jit(solution)/shard_map/ppermute | solution.py:190
  6.0 1.4 %collective-permute-start.1 = (f32[256,128]{1,0:T(8,128)S(1)}, f32[256,128]{1,0:T(8,128)S(1)}, u32[]{:S(2)}, u32[]{:S(2)}) collective-permute-start(f32[256,128]{1,0:T(8,128)S(1)} %get-tuple-element.17), channel_id=1, source_target_pairs={{0,1},{1,0},{2,3},{3,2},{4,5},{5,4},{6,7},{7,6},{8,9},{9,8},{10,11... | collective-permute-start | bytes 393224 | tf_op jit(solution)/shard_map/ppermute | solution.py:194
  7.4 1.3 %collective-permute-start.2 = (f32[128,128]{1,0:T(8,128)S(1)}, f32[128,128]{1,0:T(8,128)S(1)}, u32[]{:S(2)}, u32[]{:S(2)}) collective-permute-start(f32[128,128]{1,0:T(8,128)S(1)} %fusion), channel_id=1, source_target_pairs={{0,1},{1,0},{2,3},{3,2},{4,5},{5,4},{6,7},{7,6},{8,9},{9,8},{10,11... | collective-permute-start | bytes 196616 | tf_op jit(solution)/shard_map/ppermute | solution.py:197
  8.9 5.6 %collective-permute-start.3 = (f32[128,256]{1,0:T(8,128)S(1)}, f32[128,256]{1,0:T(8,128)S(1)}, u32[]{:S(2)}, u32[]{:S(2)}) collective-permute-start(f32[128,256]{1,0:T(8,128)S(1)} %pad_maximum_fusion.own), channel_id=1, source_target_pairs={{0,2},{2,0},{4,6},{6,4},{8,10},{10,8},{12,14},{14,12},{1,3},{3,1},... | collective-permute-start | bytes 393224 | tf_op jit(solution)/shard_map/ppermute | solution.py:210
  10.4 6.4 %collective-permute-start.4 = (f32[128,256]{1,0:T(8,128)S(1)}, f32[128,256]{1,0:T(8,128)S(1)}, u32[]{:S(2)}, u32[]{:S(2)}) collective-permute-start(f32[128,256]{1,0:T(8,128)S(1)} %pad_maximum_fusion.own), channel_id=1, source_target_pairs={{0,4},{2,6},{4,0},{6,2},{8,12},{10,14},{12,8},{14,10},{1,5},{3,7},... | collective-permute-start | bytes 393224 | tf_op jit(solution)/shard_map/ppermute | solution.py:210
  11.9 6.5 %collective-permute-start.5 = (f32[128,256]{1,0:T(8,128)S(1)}, f32[128,256]{1,0:T(8,128)S(1)}, u32[]{:S(2)}, u32[]{:S(2)}) collective-permute-start(f32[128,256]{1,0:T(8,128)S(1)} %pad_maximum_fusion.own), channel_id=1, source_target_pairs={{0,6},{2,4},{4,2},{6,0},{8,14},{10,12},{12,10},{14,8},{1,7},{3,5},... | collective-permute-start | bytes 393224 | tf_op jit(solution)/shard_map/ppermute | solution.py:210
  18.9 5.2 %collective-permute-start.6 = (f32[128,128]{1,0:T(8,128)S(1)}, f32[128,128]{1,0:T(8,128)S(1)}, u32[]{:S(2)}, u32[]{:S(2)}) collective-permute-start(f32[128,128]{1,0:T(8,128)S(1)} %shard_map.87.after), channel_id=1, source_target_pairs={{0,8},{2,10},{4,12},{6,14},{8,0},{10,2},{12,4},{14,6},{1,9},{3,11}... | collective-permute-start | bytes 196616 | tf_op jit(solution)/shard_map/ppermute | solution.py:210

commit v7 on v6

--- a/solution.py
+++ b/solution.py
@@ -118,11 +118,10 @@
 
 
 def product(a, b):
-    def dot(x, y):
-        return jnp.dot(x, y, preferred_element_type=jnp.float32)
-
     (ah, al), (bh, bl) = split(a), split(b)
-    return dot(ah, bh) + (dot(ah, bl) + dot(al, bh))
+    wide = jnp.concatenate([ah, ah, al], 1)
+    tall = jnp.concatenate([bh, bl, bh], 0)
+    return jnp.dot(wide, tall, preferred_element_type=jnp.float32)
 
 
 def top_kernel(own, near, across, far, out):

time: 24.3 us -> 24.3 us (level)
  no operation moved by 1% of the time
where the time goes in v7:
time: 24.3 us; the launch traced here: 24.1 us
  starting transfers between devices  9.41 us (39%)
  waiting for transfers between devices  8.34 us (34%)
  Pallas kernels  4.38 us (18%)
  matrix products  1.14 us (5%)
  between operations  0.76 us (3%)
    ppermute x4, starting transfers between devices, swap(): return lax.ppermute(array, 'pcol', pairs)  6.21 us
    ppermute x4, waiting for transfers between devices, swap(): return lax.ppermute(array, 'pcol', pairs)  6.11 us
    ppermute x1, starting transfers between devices, on_device(): ahead = lax.ppermute(sep_coupling[0], ('pcol', 'prow'), shift)  2.99 us
    pallas_call x1, Pallas kernels, leaves(): pl.pallas_call(leaf_kernel, out_shape=(pltpu.VMEM(rhs.shape, jnp.bfloat16...  2.35 us
    pallas_call x2, Pallas kernels, store(): pl.pallas_call(store_kernel, out_shape=pltpu.HBM(array.shape, array.dtype...  1.62 us
    dot_general x6, matrix products, mul(): return jnp.dot(a, b, precision=lax.Precision.HIGH)  1.14 us
    ppermute x1, waiting for transfers between devices, on_device(): other_b = lax.ppermute(b, 'prow', [(0, 1), (1, 0)])  1.09 us
    ppermute x1, waiting for transfers between devices, on_device(): came = lax.ppermute(sent, 'prow', [(0, 1), (1, 0)])  1.02 us
  transfers between devices with their start and end apart: 7, of which 6 were waited for; matrix products, arithmetic and copies ran while one was open for 4% of the time, Pallas kernels for 16%

profile of v7, /device:TPU:0, one launch (start us, length us, event | category | flops | bytes accessed | tf_op | source)
XLA Modules:
  0.0 24.1 jit_solution(10547276538226150431)
XLA Ops:
  0.6 3.0 %collective-permute-start = (f32[128,128]{1,0:T(8,128)}, f32[128,128]{1,0:T(8,128)S(1)}, u32[]{:S(2)}, u32[]{:S(2)}) collective-permute-start(f32[128,128]{1,0:T(8,128)} %bitcast.11), channel_id=1, source_target_pairs={{0,2},{2,0},{4,6},{6,4},{8,10},{10,8},{12,14},{14,12},{5,3},{3,1},... | collective-permute-start | bytes 196616 | tf_op jit(solution)/shard_map/ppermute | solution.py:189
  3.6 2.4 %shard_map.86 = (bf16[2048,256]{1,0:T(8,128)(2,1)S(1)}, f32[256,128]{1,0:T(8,128)S(1)}, f32[256,128]{1,0:T(8,128)S(1)}, f32[128,128]{1,0:T(8,128)S(1)}) custom-call(s32[16]{0:T(128)} %parent_in.1, bf16[16,128,128]{2,1,0:T(8,128)(2,1)} %inverse_in.1, bf16[2048,256]{1,0:T(8,128)(2,1)} %rhs_in.1, bf16[128,2048]{1,0:T(8,128)(2,1)} %coupling_in.1, ...), custom_call_target="tpu_custom_call" | custom-call | tf_op jit(solution)/shard_map/pallas_call | solution.py:80
  6.0 0.1 collective-permute-start.1
  6.1 0.1 collective-permute-done
  6.2 0.2 fusion
  6.4 1.0 %collective-permute-done.1 = f32[256,128]{1,0:T(8,128)S(1)} collective-permute-done((f32[256,128]{1,0:T(8,128)S(1)}, f32[256,128]{1,0:T(8,128)S(1)}, u32[]{:S(2)}, u32[]{:S(2)}) %collective-permute-start.1) | collective-permute-done | bytes 131104 | tf_op jit(solution)/shard_map/ppermute | solution.py:193
  7.4 0.1 collective-permute-start.2
  7.6 1.1 %collective-permute-done.2 = f32[128,128]{1,0:T(8,128)S(1)} collective-permute-done((f32[128,128]{1,0:T(8,128)S(1)}, f32[128,128]{1,0:T(8,128)S(1)}, u32[]{:S(2)}, u32[]{:S(2)}) %collective-permute-start.2) | collective-permute-done | bytes 65568 | tf_op jit(solution)/shard_map/ppermute | solution.py:196
  8.7 0.2 convolution_add_fusion
  8.9 1.5 %collective-permute-start.3 = (f32[128,256]{1,0:T(8,128)S(1)}, f32[128,256]{1,0:T(8,128)S(1)}, u32[]{:S(2)}, u32[]{:S(2)}) collective-permute-start(f32[128,256]{1,0:T(8,128)S(1)} %pad_maximum_fusion.own), channel_id=1, source_target_pairs={{0,2},{2,0},{4,6},{6,4},{8,10},{10,8},{12,14},{14,12},{1,3},{3,1},... | collective-permute-start | bytes 393224 | tf_op jit(solution)/shard_map/ppermute | solution.py:209
  10.4 1.6 %collective-permute-start.4 = (f32[128,256]{1,0:T(8,128)S(1)}, f32[128,256]{1,0:T(8,128)S(1)}, u32[]{:S(2)}, u32[]{:S(2)}) collective-permute-start(f32[128,256]{1,0:T(8,128)S(1)} %pad_maximum_fusion.own), channel_id=1, source_target_pairs={{0,4},{2,6},{4,0},{6,2},{8,12},{10,14},{12,8},{14,10},{1,5},{3,7},... | collective-permute-start | bytes 393224 | tf_op jit(solution)/shard_map/ppermute | solution.py:209
  11.9 0.5 %collective-permute-start.5 = (f32[128,256]{1,0:T(8,128)S(1)}, f32[128,256]{1,0:T(8,128)S(1)}, u32[]{:S(2)}, u32[]{:S(2)}) collective-permute-start(f32[128,256]{1,0:T(8,128)S(1)} %pad_maximum_fusion.own), channel_id=1, source_target_pairs={{0,6},{2,4},{4,2},{6,0},{8,14},{10,12},{12,10},{14,8},{1,7},{3,5},... | collective-permute-start | bytes 393224 | tf_op jit(solution)/shard_map/ppermute | solution.py:209
  12.4 2.1 %collective-permute-done.3.near = f32[128,256]{1,0:T(8,128)S(1)} collective-permute-done((f32[128,256]{1,0:T(8,128)S(1)}, f32[128,256]{1,0:T(8,128)S(1)}, u32[]{:S(2)}, u32[]{:S(2)}) %collective-permute-start.3) | collective-permute-done | bytes 131104 | tf_op jit(solution)/shard_map/ppermute | solution.py:209
  14.5 2.3 %collective-permute-done.4.across = f32[128,256]{1,0:T(8,128)S(1)} collective-permute-done((f32[128,256]{1,0:T(8,128)S(1)}, f32[128,256]{1,0:T(8,128)S(1)}, u32[]{:S(2)}, u32[]{:S(2)}) %collective-permute-start.4) | collective-permute-done | bytes 131104 | tf_op jit(solution)/shard_map/ppermute | solution.py:209
  16.7 1.7 %collective-permute-done.5.far = f32[128,256]{1,0:T(8,128)S(1)} collective-permute-done((f32[128,256]{1,0:T(8,128)S(1)}, f32[128,256]{1,0:T(8,128)S(1)}, u32[]{:S(2)}, u32[]{:S(2)}) %collective-permute-start.5) | collective-permute-done | bytes 131104 | tf_op jit(solution)/shard_map/ppermute | solution.py:209
  18.5 0.4 %shard_map.87.after = f32[128,128]{1,0:T(8,128)S(1)} custom-call(f32[128,256]{1,0:T(8,128)S(1)} %pad_maximum_fusion.own, f32[128,256]{1,0:T(8,128)S(1)} %collective-permute-done.3.near, f32[128,256]{1,0:T(8,128)S(1)} %collective-permute-done.4.across, f32[128,256]{1,0:T(8,128)S(1)} %collective-permute-done.5.far), custom_call_target="tpu_custom_call" | custom-call | bytes 65536 | tf_op jit(solution)/shard_map/pallas_call | solution.py:146
  18.9 2.7 %collective-permute-start.6 = (f32[128,128]{1,0:T(8,128)S(1)}, f32[128,128]{1,0:T(8,128)S(1)}, u32[]{:S(2)}, u32[]{:S(2)}) collective-permute-start(f32[128,128]{1,0:T(8,128)S(1)} %shard_map.87.after), channel_id=1, source_target_pairs={{0,8},{2,10},{4,12},{6,14},{8,0},{10,2},{12,4},{14,6},{1,9},{3,11}... | collective-permute-start | bytes 196616 | tf_op jit(solution)/shard_map/ppermute | solution.py:209
  21.5 0.2 fusion.12
  21.8 0.2 fusion.5
  22.0 0.2 fusion.1
  22.2 0.2 subtract_select_fusion.solved.found
  22.4 0.6 %shard_map.89.written = f32[128,128]{1,0:T(8,128)} custom-call(f32[128,128]{1,0:T(8,128)S(1)} %subtract_select_fusion.solved.found, f32[128,128]{1,0:T(8,128)S(1)} %slice_select_fusion.after.weight), custom_call_target="tpu_custom_call" | custom-call | bytes 65536 | tf_op jit(solution)/shard_map/pallas_call | solution.py:105
  23.1 1.0 %shard_map.88 = bf16[2048,256]{1,0:T(8,128)(2,1)} custom-call(bf16[2048,256]{1,0:T(8,128)(2,1)S(1)} %get-tuple-element.15.solved, f32[128,128]{1,0:T(8,128)S(1)} %shard_map.87.after), custom_call_target="tpu_custom_call" | custom-call | bytes 65536 | tf_op jit(solution)/shard_map/pallas_call | solution.py:105
  24.1 0.0 collective-permute-done.6.came
  (7 shorter events, 0.1 us)
Async XLA Ops:
  0.6 5.6 %collective-permute-start = (f32[128,128]{1,0:T(8,128)}, f32[128,128]{1,0:T(8,128)S(1)}, u32[]{:S(2)}, u32[]{:S(2)}) collective-permute-start(f32[128,128]{1,0:T(8,128)} %bitcast.11), channel_id=1, source_target_pairs={{0,2},{2,0},{4,6},{6,4},{8,10},{10,8},{12,14},{14,12},{5,3},{3,1},... | collective-permute-start | bytes 196616 | tf_op jit(solution)/shard_map/ppermute | solution.py:189
  6.0 1.4 %collective-permute-start.1 = (f32[256,128]{1,0:T(8,128)S(1)}, f32[256,128]{1,0:T(8,128)S(1)}, u32[]{:S(2)}, u32[]{:S(2)}) collective-permute-start(f32[256,128]{1,0:T(8,128)S(1)} %get-tuple-element.17), channel_id=1, source_target_pairs={{0,1},{1,0},{2,3},{3,2},{4,5},{5,4},{6,7},{7,6},{8,9},{9,8},{10,11... | collective-permute-start | bytes 393224 | tf_op jit(solution)/shard_map/ppermute | solution.py:193
  7.4 1.3 %collective-permute-start.2 = (f32[128,128]{1,0:T(8,128)S(1)}, f32[128,128]{1,0:T(8,128)S(1)}, u32[]{:S(2)}, u32[]{:S(2)}) collective-permute-start(f32[128,128]{1,0:T(8,128)S(1)} %fusion), channel_id=1, source_target_pairs={{0,1},{1,0},{2,3},{3,2},{4,5},{5,4},{6,7},{7,6},{8,9},{9,8},{10,11... | collective-permute-start | bytes 196616 | tf_op jit(solution)/shard_map/ppermute | solution.py:196
  8.9 5.6 %collective-permute-start.3 = (f32[128,256]{1,0:T(8,128)S(1)}, f32[128,256]{1,0:T(8,128)S(1)}, u32[]{:S(2)}, u32[]{:S(2)}) collective-permute-start(f32[128,256]{1,0:T(8,128)S(1)} %pad_maximum_fusion.own), channel_id=1, source_target_pairs={{0,2},{2,0},{4,6},{6,4},{8,10},{10,8},{12,14},{14,12},{1,3},{3,1},... | collective-permute-start | bytes 393224 | tf_op jit(solution)/shard_map/ppermute | solution.py:209
  10.4 6.4 %collective-permute-start.4 = (f32[128,256]{1,0:T(8,128)S(1)}, f32[128,256]{1,0:T(8,128)S(1)}, u32[]{:S(2)}, u32[]{:S(2)}) collective-permute-start(f32[128,256]{1,0:T(8,128)S(1)} %pad_maximum_fusion.own), channel_id=1, source_target_pairs={{0,4},{2,6},{4,0},{6,2},{8,12},{10,14},{12,8},{14,10},{1,5},{3,7},... | collective-permute-start | bytes 393224 | tf_op jit(solution)/shard_map/ppermute | solution.py:209
  11.9 6.5 %collective-permute-start.5 = (f32[128,256]{1,0:T(8,128)S(1)}, f32[128,256]{1,0:T(8,128)S(1)}, u32[]{:S(2)}, u32[]{:S(2)}) collective-permute-start(f32[128,256]{1,0:T(8,128)S(1)} %pad_maximum_fusion.own), channel_id=1, source_target_pairs={{0,6},{2,4},{4,2},{6,0},{8,14},{10,12},{12,10},{14,8},{1,7},{3,5},... | collective-permute-start | bytes 393224 | tf_op jit(solution)/shard_map/ppermute | solution.py:209
  18.9 5.2 %collective-permute-start.6 = (f32[128,128]{1,0:T(8,128)S(1)}, f32[128,128]{1,0:T(8,128)S(1)}, u32[]{:S(2)}, u32[]{:S(2)}) collective-permute-start(f32[128,128]{1,0:T(8,128)S(1)} %shard_map.87.after), channel_id=1, source_target_pairs={{0,8},{2,10},{4,12},{6,14},{8,0},{10,2},{12,4},{14,6},{1,9},{3,11}... | collective-permute-start | bytes 196616 | tf_op jit(solution)/shard_map/ppermute | solution.py:209

commit v8 on v7

--- a/solution.py
+++ b/solution.py
@@ -209,9 +209,19 @@
         return lax.ppermute(array, "pcol", pairs)
 
     flights = {}
-    order = (1, 2, 3)
-    arrived = lax.optimization_barrier([swap(total, d) for d in order])
-    flights = dict(zip(order, arrived))
+    def mixed(first, second):
+        pairs = [
+            (2 * i + r, 2 * (i ^ d) + r)
+            for i in range(columns)
+            for r, d in ((0, first), (1, second))
+            if i ^ d < columns
+        ]
+        return lax.ppermute(total, ("pcol", "prow"), pairs)
+
+    arrived = lax.optimization_barrier([mixed(*(1, 2)), mixed(*(2, 1)), mixed(*(3, 3))])
+    flights = {}
+    for d in (1, 2, 3):
+        flights[d] = jnp.where(row == 0, arrived[{1: 0, 2: 1, 3: 2}[d]], arrived[{2: 0, 1: 1, 3: 2}[d]])
     odd = (column & 1) != 0
 
     def other_pair(pieces):

time: 24.3 us -> 24 us (0.988)
  waiting for transfers between devices: 8.34 us -> 8.03 us
    ppermute x4 -> x1, waiting for transfers between devices: 6.11 us -> 0.05 us  [swap(): return lax.ppermute(array, 'pcol', pairs)]
    ppermute x0 -> x3, waiting for transfers between devices: none -> 5.75 us  [mixed(): return lax.ppermute(total, ('pcol', 'prow'), pairs)]
    ppermute x0 -> x3, starting transfers between devices: none -> 3.55 us  [mixed(): return lax.ppermute(total, ('pcol', 'prow'), pairs)]
    ppermute x4 -> x1, starting transfers between devices: 6.21 us -> 2.65 us  [swap(): return lax.ppermute(array, 'pcol', pairs)]
  transfers between devices with their start and end apart: 7 -> 7, of which waited for: 6 -> 6; matrix products, arithmetic and copies ran while one was open for 4% -> 4% of each run, Pallas kernels for 16% -> 17%
where the time goes in v8:
time: 24 us; the launch traced here: 23.8 us
  starting transfers between devices  9.42 us (39%)
  waiting for transfers between devices  8.03 us (33%)
  Pallas kernels  4.38 us (18%)
  matrix products  1.14 us (5%)
  between operations  0.77 us (3%)
    ppermute x3, waiting for transfers between devices, mixed(): return lax.ppermute(total, ('pcol', 'prow'), pairs)  5.75 us
    ppermute x3, starting transfers between devices, mixed(): return lax.ppermute(total, ('pcol', 'prow'), pairs)  3.55 us
    ppermute x1, starting transfers between devices, on_device(): ahead = lax.ppermute(sep_coupling[0], ('pcol', 'prow'), shift)  2.99 us
    ppermute x1, starting transfers between devices, swap(): return lax.ppermute(array, 'pcol', pairs)  2.65 us
    pallas_call x1, Pallas kernels, leaves(): pl.pallas_call(leaf_kernel, out_shape=(pltpu.VMEM(rhs.shape, jnp.bfloat16...  2.35 us
    pallas_call x2, Pallas kernels, store(): pl.pallas_call(store_kernel, out_shape=pltpu.HBM(array.shape, array.dtype...  1.62 us
    dot_general x6, matrix products, mul(): return jnp.dot(a, b, precision=lax.Precision.HIGH)  1.14 us
    ppermute x1, waiting for transfers between devices, on_device(): other_b = lax.ppermute(b, 'prow', [(0, 1), (1, 0)])  1.09 us
  transfers between devices with their start and end apart: 7, of which 6 were waited for; matrix products, arithmetic and copies ran while one was open for 4% of the time, Pallas kernels for 17%

profile of v8, /device:TPU:0, one launch (start us, length us, event | category | flops | bytes accessed | tf_op | source)
XLA Modules:
  0.0 23.8 jit_solution(8291324016880803033)
XLA Ops:
  0.6 3.0 %collective-permute-start = (f32[128,128]{1,0:T(8,128)}, f32[128,128]{1,0:T(8,128)S(1)}, u32[]{:S(2)}, u32[]{:S(2)}) collective-permute-start(f32[128,128]{1,0:T(8,128)} %bitcast.11), channel_id=1, source_target_pairs={{0,2},{2,0},{4,6},{6,4},{8,10},{10,8},{12,14},{14,12},{5,3},{3,1},... | collective-permute-start | bytes 196616 | tf_op jit(solution)/shard_map/ppermute | solution.py:189
  3.6 2.4 %shard_map.86 = (bf16[2048,256]{1,0:T(8,128)(2,1)S(1)}, f32[256,128]{1,0:T(8,128)S(1)}, f32[256,128]{1,0:T(8,128)S(1)}, f32[128,128]{1,0:T(8,128)S(1)}) custom-call(s32[16]{0:T(128)} %parent_in.1, bf16[16,128,128]{2,1,0:T(8,128)(2,1)} %inverse_in.1, bf16[2048,256]{1,0:T(8,128)(2,1)} %rhs_in.1, bf16[128,2048]{1,0:T(8,128)(2,1)} %coupling_in.1, ...), custom_call_target="tpu_custom_call" | custom-call | tf_op jit(solution)/shard_map/pallas_call | solution.py:80
  6.0 0.1 collective-permute-start.1
  6.1 0.1 collective-permute-done
  6.2 0.2 fusion
  6.4 1.0 %collective-permute-done.1 = f32[256,128]{1,0:T(8,128)S(1)} collective-permute-done((f32[256,128]{1,0:T(8,128)S(1)}, f32[256,128]{1,0:T(8,128)S(1)}, u32[]{:S(2)}, u32[]{:S(2)}) %collective-permute-start.1) | collective-permute-done | bytes 131104 | tf_op jit(solution)/shard_map/ppermute | solution.py:193
  7.4 0.1 collective-permute-start.2
  7.6 1.1 %collective-permute-done.2 = f32[128,128]{1,0:T(8,128)S(1)} collective-permute-done((f32[128,128]{1,0:T(8,128)S(1)}, f32[128,128]{1,0:T(8,128)S(1)}, u32[]{:S(2)}, u32[]{:S(2)}) %collective-permute-start.2) | collective-permute-done | bytes 65568 | tf_op jit(solution)/shard_map/ppermute | solution.py:196
  8.7 0.2 convolution_add_fusion
  8.9 1.5 %collective-permute-start.3 = (f32[128,256]{1,0:T(8,128)S(1)}, f32[128,256]{1,0:T(8,128)S(1)}, u32[]{:S(2)}, u32[]{:S(2)}) collective-permute-start(f32[128,256]{1,0:T(8,128)S(1)} %pad_maximum_fusion.own), channel_id=1, source_target_pairs={{0,2},{1,5},{2,0},{3,7},{4,6},{5,1},{6,4},{7,3},{8,10},{9,13},{10,... | collective-permute-start | bytes 393224 | tf_op jit(solution)/shard_map/ppermute | solution.py:219
  10.4 1.6 %collective-permute-start.4 = (f32[128,256]{1,0:T(8,128)S(1)}, f32[128,256]{1,0:T(8,128)S(1)}, u32[]{:S(2)}, u32[]{:S(2)}) collective-permute-start(f32[128,256]{1,0:T(8,128)S(1)} %pad_maximum_fusion.own), channel_id=1, source_target_pairs={{0,4},{1,3},{2,6},{3,1},{4,0},{5,7},{6,2},{7,5},{8,12},{9,11},{10,... | collective-permute-start | bytes 393224 | tf_op jit(solution)/shard_map/ppermute | solution.py:219
  11.9 0.5 %collective-permute-start.5 = (f32[128,256]{1,0:T(8,128)S(1)}, f32[128,256]{1,0:T(8,128)S(1)}, u32[]{:S(2)}, u32[]{:S(2)}) collective-permute-start(f32[128,256]{1,0:T(8,128)S(1)} %pad_maximum_fusion.own), channel_id=1, source_target_pairs={{0,6},{1,7},{2,4},{3,5},{4,2},{5,3},{6,0},{7,1},{8,14},{9,15},{10,... | collective-permute-start | bytes 393224 | tf_op jit(solution)/shard_map/ppermute | solution.py:219
  12.4 2.5 %collective-permute-done.3 = f32[128,256]{1,0:T(8,128)S(1)} collective-permute-done((f32[128,256]{1,0:T(8,128)S(1)}, f32[128,256]{1,0:T(8,128)S(1)}, u32[]{:S(2)}, u32[]{:S(2)}) %collective-permute-start.3) | collective-permute-done | bytes 131104 | tf_op jit(solution)/shard_map/ppermute | solution.py:219
  14.9 1.6 %collective-permute-done.4 = f32[128,256]{1,0:T(8,128)S(1)} collective-permute-done((f32[128,256]{1,0:T(8,128)S(1)}, f32[128,256]{1,0:T(8,128)S(1)}, u32[]{:S(2)}, u32[]{:S(2)}) %collective-permute-start.4) | collective-permute-done | bytes 131104 | tf_op jit(solution)/shard_map/ppermute | solution.py:219
  16.5 1.7 %collective-permute-done.5.far = f32[128,256]{1,0:T(8,128)S(1)} collective-permute-done((f32[128,256]{1,0:T(8,128)S(1)}, f32[128,256]{1,0:T(8,128)S(1)}, u32[]{:S(2)}, u32[]{:S(2)}) %collective-permute-start.5) | collective-permute-done | bytes 131104 | tf_op jit(solution)/shard_map/ppermute | solution.py:219
  18.2 0.4 %shard_map.87.after = f32[128,128]{1,0:T(8,128)S(1)} custom-call(f32[128,256]{1,0:T(8,128)S(1)} %pad_maximum_fusion.own, f32[128,256]{1,0:T(8,128)S(1)} %get-tuple-element.25.near, f32[128,256]{1,0:T(8,128)S(1)} %get-tuple-element.26.across, f32[128,256]{1,0:T(8,128)S(1)} %collective-permute-done.5.far), custom_call_target="tpu_custom_call" | custom-call | bytes 65536 | tf_op jit(solution)/shard_map/pallas_call | solution.py:146
  18.6 2.7 %collective-permute-start.6 = (f32[128,128]{1,0:T(8,128)S(1)}, f32[128,128]{1,0:T(8,128)S(1)}, u32[]{:S(2)}, u32[]{:S(2)}) collective-permute-start(f32[128,128]{1,0:T(8,128)S(1)} %shard_map.87.after), channel_id=1, source_target_pairs={{0,8},{2,10},{4,12},{6,14},{8,0},{10,2},{12,4},{14,6},{1,9},{3,11}... | collective-permute-start | bytes 196616 | tf_op jit(solution)/shard_map/ppermute | solution.py:209
  21.3 0.2 fusion.12
  21.5 0.2 fusion.5
  21.7 0.2 fusion.1
  21.9 0.2 subtract_select_fusion.solved.found
  22.1 0.6 %shard_map.89.written = f32[128,128]{1,0:T(8,128)} custom-call(f32[128,128]{1,0:T(8,128)S(1)} %subtract_select_fusion.solved.found, f32[128,128]{1,0:T(8,128)S(1)} %slice_select_fusion.after.weight), custom_call_target="tpu_custom_call" | custom-call | bytes 65536 | tf_op jit(solution)/shard_map/pallas_call | solution.py:105
  22.8 1.0 %shard_map.88 = bf16[2048,256]{1,0:T(8,128)(2,1)} custom-call(bf16[2048,256]{1,0:T(8,128)(2,1)S(1)} %get-tuple-element.15.solved, f32[128,128]{1,0:T(8,128)S(1)} %shard_map.87.after), custom_call_target="tpu_custom_call" | custom-call | bytes 65536 | tf_op jit(solution)/shard_map/pallas_call | solution.py:105
  23.8 0.0 collective-permute-done.6.came
  (8 shorter events, 0.1 us)
Async XLA Ops:
  0.6 5.6 %collective-permute-start = (f32[128,128]{1,0:T(8,128)}, f32[128,128]{1,0:T(8,128)S(1)}, u32[]{:S(2)}, u32[]{:S(2)}) collective-permute-start(f32[128,128]{1,0:T(8,128)} %bitcast.11), channel_id=1, source_target_pairs={{0,2},{2,0},{4,6},{6,4},{8,10},{10,8},{12,14},{14,12},{5,3},{3,1},... | collective-permute-start | bytes 196616 | tf_op jit(solution)/shard_map/ppermute | solution.py:189
  6.0 1.4 %collective-permute-start.1 = (f32[256,128]{1,0:T(8,128)S(1)}, f32[256,128]{1,0:T(8,128)S(1)}, u32[]{:S(2)}, u32[]{:S(2)}) collective-permute-start(f32[256,128]{1,0:T(8,128)S(1)} %get-tuple-element.17), channel_id=1, source_target_pairs={{0,1},{1,0},{2,3},{3,2},{4,5},{5,4},{6,7},{7,6},{8,9},{9,8},{10,11... | collective-permute-start | bytes 393224 | tf_op jit(solution)/shard_map/ppermute | solution.py:193
  7.4 1.3 %collective-permute-start.2 = (f32[128,128]{1,0:T(8,128)S(1)}, f32[128,128]{1,0:T(8,128)S(1)}, u32[]{:S(2)}, u32[]{:S(2)}) collective-permute-start(f32[128,128]{1,0:T(8,128)S(1)} %fusion), channel_id=1, source_target_pairs={{0,1},{1,0},{2,3},{3,2},{4,5},{5,4},{6,7},{7,6},{8,9},{9,8},{10,11... | collective-permute-start | bytes 196616 | tf_op jit(solution)/shard_map/ppermute | solution.py:196
  8.9 6.0 %collective-permute-start.3 = (f32[128,256]{1,0:T(8,128)S(1)}, f32[128,256]{1,0:T(8,128)S(1)}, u32[]{:S(2)}, u32[]{:S(2)}) collective-permute-start(f32[128,256]{1,0:T(8,128)S(1)} %pad_maximum_fusion.own), channel_id=1, source_target_pairs={{0,2},{1,5},{2,0},{3,7},{4,6},{5,1},{6,4},{7,3},{8,10},{9,13},{10,... | collective-permute-start | bytes 393224 | tf_op jit(solution)/shard_map/ppermute | solution.py:219
  10.4 6.1 %collective-permute-start.4 = (f32[128,256]{1,0:T(8,128)S(1)}, f32[128,256]{1,0:T(8,128)S(1)}, u32[]{:S(2)}, u32[]{:S(2)}) collective-permute-start(f32[128,256]{1,0:T(8,128)S(1)} %pad_maximum_fusion.own), channel_id=1, source_target_pairs={{0,4},{1,3},{2,6},{3,1},{4,0},{5,7},{6,2},{7,5},{8,12},{9,11},{10,... | collective-permute-start | bytes 393224 | tf_op jit(solution)/shard_map/ppermute | solution.py:219
  11.9 6.2 %collective-permute-start.5 = (f32[128,256]{1,0:T(8,128)S(1)}, f32[128,256]{1,0:T(8,128)S(1)}, u32[]{:S(2)}, u32[]{:S(2)}) collective-permute-start(f32[128,256]{1,0:T(8,128)S(1)} %pad_maximum_fusion.own), channel_id=1, source_target_pairs={{0,6},{1,7},{2,4},{3,5},{4,2},{5,3},{6,0},{7,1},{8,14},{9,15},{10,... | collective-permute-start | bytes 393224 | tf_op jit(solution)/shard_map/ppermute | solution.py:219
  18.6 5.2 %collective-permute-start.6 = (f32[128,128]{1,0:T(8,128)S(1)}, f32[128,128]{1,0:T(8,128)S(1)}, u32[]{:S(2)}, u32[]{:S(2)}) collective-permute-start(f32[128,128]{1,0:T(8,128)S(1)} %shard_map.87.after), channel_id=1, source_target_pairs={{0,8},{2,10},{4,12},{6,14},{8,0},{10,2},{12,4},{14,6},{1,9},{3,11}... | collective-permute-start | bytes 196616 | tf_op jit(solution)/shard_map/ppermute | solution.py:209

commit v9 on v8

--- a/solution.py
+++ b/solution.py
@@ -124,14 +124,18 @@
     return jnp.dot(wide, tall, preferred_element_type=jnp.float32)
 
 
-def top_kernel(own, near, across, far, out):
+def top_kernel(own, one, two, last, out):
+    zero = lax.axis_index("prow") == 0
+    near = jnp.where(zero, one[...], two[...])
+    across = jnp.where(zero, two[...], one[...])
+    far = last[...]
     column = lax.axis_index("pcol")
     odd = (column & 1) != 0
     high = (column & 2) != 0
     half = out.shape[1]
-    low_own, high_own = jnp.where(odd, near[...], own[...]), jnp.where(odd, own[...], near[...])
-    low_other = jnp.where(odd, far[...], across[...])
-    high_other = jnp.where(odd, across[...], far[...])
+    low_own, high_own = jnp.where(odd, near, own[...]), jnp.where(odd, own[...], near)
+    low_other = jnp.where(odd, far, across)
+    high_other = jnp.where(odd, across, far)
     first = jnp.where(high, low_other, low_own)
     second = jnp.where(high, high_other, high_own)
     third = jnp.where(high, low_own, low_other)
@@ -208,7 +212,6 @@
         pairs = [(i, i ^ distance) for i in range(columns) if i ^ distance < columns]
         return lax.ppermute(array, "pcol", pairs)
 
-    flights = {}
     def mixed(first, second):
         pairs = [
             (2 * i + r, 2 * (i ^ d) + r)
@@ -219,18 +222,21 @@
         return lax.ppermute(total, ("pcol", "prow"), pairs)
 
     arrived = lax.optimization_barrier([mixed(*(1, 2)), mixed(*(2, 1)), mixed(*(3, 3))])
-    flights = {}
-    for d in (1, 2, 3):
-        flights[d] = jnp.where(row == 0, arrived[{1: 0, 2: 1, 3: 2}[d]], arrived[{2: 0, 1: 1, 3: 2}[d]])
     odd = (column & 1) != 0
+
+    def pieces(came):
+        near = jnp.where(row == 0, came[0], came[1])
+        across = jnp.where(row == 0, came[1], came[0])
+        return {1: near, 2: across, 3: came[2]}
 
     def other_pair(pieces):
         return join(jnp.where(odd, pieces[3], pieces[2]), jnp.where(odd, pieces[2], pieces[3]))
 
     if columns == 8:
-        total = top(total, flights[1], flights[2], flights[3])
+        total = top(total, *arrived)
         late = ()
     else:
+        flights = pieces(arrived)
         late = ((1, flights[1]), (2, other_pair(flights)))
         for distance, came in late:
             upper = (column & distance) != 0
@@ -244,8 +250,9 @@
         distance *= 2
     total = total[:, :half]
     came = swap(total, distance)
-    flights, late, total = lax.optimization_barrier((flights, late, total))
+    arrived, late, total = lax.optimization_barrier((arrived, late, total))
     if columns == 8:
+        flights = pieces(arrived)
         late = ((1, flights[1]), (2, other_pair(flights)))
     for place, block_came in late:
         above = (column & place) != 0

time: 24 us -> 24 us (level)
  no operation moved by 1% of the time
where the time goes in v9:
time: 24 us; the launch traced here: 23.8 us
  starting transfers between devices  9.42 us (39%)
  waiting for transfers between devices  8.02 us (33%)
  Pallas kernels  4.38 us (18%)
  matrix products  1.15 us (5%)
  between operations  0.76 us (3%)
    ppermute x3, waiting for transfers between devices, mixed(): return lax.ppermute(total, ('pcol', 'prow'), pairs)  5.75 us
    ppermute x3, starting transfers between devices, mixed(): return lax.ppermute(total, ('pcol', 'prow'), pairs)  3.55 us
    ppermute x1, starting transfers between devices, on_device(): ahead = lax.ppermute(sep_coupling[0], ('pcol', 'prow'), shift)  2.99 us
    ppermute x1, starting transfers between devices, swap(): return lax.ppermute(array, 'pcol', pairs)  2.66 us
    pallas_call x1, Pallas kernels, leaves(): pl.pallas_call(leaf_kernel, out_shape=(pltpu.VMEM(rhs.shape, jnp.bfloat16...  2.35 us
    pallas_call x2, Pallas kernels, store(): pl.pallas_call(store_kernel, out_shape=pltpu.HBM(array.shape, array.dtype...  1.62 us
    dot_general x6, matrix products, mul(): return jnp.dot(a, b, precision=lax.Precision.HIGH)  1.15 us
    ppermute x1, waiting for transfers between devices, on_device(): other_b = lax.ppermute(b, 'prow', [(0, 1), (1, 0)])  1.09 us
  transfers between devices with their start and end apart: 7, of which 6 were waited for; matrix products, arithmetic and copies ran while one was open for 4% of the time, Pallas kernels for 17%

profile of v9, /device:TPU:0, one launch (start us, length us, event | category | flops | bytes accessed | tf_op | source)
XLA Modules:
  0.0 23.8 jit_solution(1944649950135259828)
XLA Ops:
  0.6 3.0 %collective-permute-start = (f32[128,128]{1,0:T(8,128)}, f32[128,128]{1,0:T(8,128)S(1)}, u32[]{:S(2)}, u32[]{:S(2)}) collective-permute-start(f32[128,128]{1,0:T(8,128)} %bitcast.10), channel_id=1, source_target_pairs={{0,2},{2,0},{4,6},{6,4},{8,10},{10,8},{12,14},{14,12},{5,3},{3,1},... | collective-permute-start | bytes 196616 | tf_op jit(solution)/shard_map/ppermute | solution.py:193
  3.6 2.4 %shard_map.86 = (bf16[2048,256]{1,0:T(8,128)(2,1)S(1)}, f32[256,128]{1,0:T(8,128)S(1)}, f32[256,128]{1,0:T(8,128)S(1)}, f32[128,128]{1,0:T(8,128)S(1)}) custom-call(s32[16]{0:T(128)} %parent_in.1, bf16[16,128,128]{2,1,0:T(8,128)(2,1)} %inverse_in.1, bf16[2048,256]{1,0:T(8,128)(2,1)} %rhs_in.1, bf16[128,2048]{1,0:T(8,128)(2,1)} %coupling_in.1, ...), custom_call_target="tpu_custom_call" | custom-call | tf_op jit(solution)/shard_map/pallas_call | solution.py:80
  6.0 0.1 collective-permute-start.1
  6.1 0.1 collective-permute-done
  6.2 0.2 fusion
  6.4 1.0 %collective-permute-done.1 = f32[256,128]{1,0:T(8,128)S(1)} collective-permute-done((f32[256,128]{1,0:T(8,128)S(1)}, f32[256,128]{1,0:T(8,128)S(1)}, u32[]{:S(2)}, u32[]{:S(2)}) %collective-permute-start.1) | collective-permute-done | bytes 131104 | tf_op jit(solution)/shard_map/ppermute | solution.py:197
  7.4 0.1 collective-permute-start.2
  7.6 1.1 %collective-permute-done.2 = f32[128,128]{1,0:T(8,128)S(1)} collective-permute-done((f32[128,128]{1,0:T(8,128)S(1)}, f32[128,128]{1,0:T(8,128)S(1)}, u32[]{:S(2)}, u32[]{:S(2)}) %collective-permute-start.2) | collective-permute-done | bytes 65568 | tf_op jit(solution)/shard_map/ppermute | solution.py:200
  8.7 0.2 convolution_add_fusion
  8.9 1.5 %collective-permute-start.3 = (f32[128,256]{1,0:T(8,128)S(1)}, f32[128,256]{1,0:T(8,128)S(1)}, u32[]{:S(2)}, u32[]{:S(2)}) collective-permute-start(f32[128,256]{1,0:T(8,128)S(1)} %pad_maximum_fusion.own), channel_id=1, source_target_pairs={{0,2},{1,5},{2,0},{3,7},{4,6},{5,1},{6,4},{7,3},{8,10},{9,13},{10,... | collective-permute-start | bytes 393224 | tf_op jit(solution)/shard_map/ppermute | solution.py:222
  10.4 1.6 %collective-permute-start.4 = (f32[128,256]{1,0:T(8,128)S(1)}, f32[128,256]{1,0:T(8,128)S(1)}, u32[]{:S(2)}, u32[]{:S(2)}) collective-permute-start(f32[128,256]{1,0:T(8,128)S(1)} %pad_maximum_fusion.own), channel_id=1, source_target_pairs={{0,4},{1,3},{2,6},{3,1},{4,0},{5,7},{6,2},{7,5},{8,12},{9,11},{10,... | collective-permute-start | bytes 393224 | tf_op jit(solution)/shard_map/ppermute | solution.py:222
  11.9 0.5 %collective-permute-start.5 = (f32[128,256]{1,0:T(8,128)S(1)}, f32[128,256]{1,0:T(8,128)S(1)}, u32[]{:S(2)}, u32[]{:S(2)}) collective-permute-start(f32[128,256]{1,0:T(8,128)S(1)} %pad_maximum_fusion.own), channel_id=1, source_target_pairs={{0,6},{1,7},{2,4},{3,5},{4,2},{5,3},{6,0},{7,1},{8,14},{9,15},{10,... | collective-permute-start | bytes 393224 | tf_op jit(solution)/shard_map/ppermute | solution.py:222
  12.4 2.5 %collective-permute-done.3.one = f32[128,256]{1,0:T(8,128)S(1)} collective-permute-done((f32[128,256]{1,0:T(8,128)S(1)}, f32[128,256]{1,0:T(8,128)S(1)}, u32[]{:S(2)}, u32[]{:S(2)}) %collective-permute-start.3) | collective-permute-done | bytes 131104 | tf_op jit(solution)/shard_map/ppermute | solution.py:222
  14.9 1.6 %collective-permute-done.4.two = f32[128,256]{1,0:T(8,128)S(1)} collective-permute-done((f32[128,256]{1,0:T(8,128)S(1)}, f32[128,256]{1,0:T(8,128)S(1)}, u32[]{:S(2)}, u32[]{:S(2)}) %collective-permute-start.4) | collective-permute-done | bytes 131104 | tf_op jit(solution)/shard_map/ppermute | solution.py:222
  16.5 1.7 %collective-permute-done.5.last = f32[128,256]{1,0:T(8,128)S(1)} collective-permute-done((f32[128,256]{1,0:T(8,128)S(1)}, f32[128,256]{1,0:T(8,128)S(1)}, u32[]{:S(2)}, u32[]{:S(2)}) %collective-permute-start.5) | collective-permute-done | bytes 131104 | tf_op jit(solution)/shard_map/ppermute | solution.py:222
  18.2 0.4 %shard_map.87.after = f32[128,128]{1,0:T(8,128)S(1)} custom-call(f32[128,256]{1,0:T(8,128)S(1)} %pad_maximum_fusion.own, f32[128,256]{1,0:T(8,128)S(1)} %collective-permute-done.3.one, f32[128,256]{1,0:T(8,128)S(1)} %collective-permute-done.4.two, f32[128,256]{1,0:T(8,128)S(1)} %collective-permute-done.5.last), custom_call_target="tpu_custom_call" | custom-call | bytes 65536 | tf_op jit(solution)/shard_map/pallas_call | solution.py:150
  18.6 2.7 %collective-permute-start.6 = (f32[128,128]{1,0:T(8,128)S(1)}, f32[128,128]{1,0:T(8,128)S(1)}, u32[]{:S(2)}, u32[]{:S(2)}) collective-permute-start(f32[128,128]{1,0:T(8,128)S(1)} %shard_map.87.after), channel_id=1, source_target_pairs={{0,8},{2,10},{4,12},{6,14},{8,0},{10,2},{12,4},{14,6},{1,9},{3,11}... | collective-permute-start | bytes 196616 | tf_op jit(solution)/shard_map/ppermute | solution.py:213
  21.2 0.2 fusion.7
  21.5 0.2 fusion.5
  21.7 0.2 fusion.1
  21.9 0.2 subtract_select_fusion.solved.found
  22.1 0.6 %shard_map.89.written = f32[128,128]{1,0:T(8,128)} custom-call(f32[128,128]{1,0:T(8,128)S(1)} %subtract_select_fusion.solved.found, f32[128,128]{1,0:T(8,128)S(1)} %slice_select_fusion.after.weight), custom_call_target="tpu_custom_call" | custom-call | bytes 65536 | tf_op jit(solution)/shard_map/pallas_call | solution.py:105
  22.8 1.0 %shard_map.88 = bf16[2048,256]{1,0:T(8,128)(2,1)} custom-call(bf16[2048,256]{1,0:T(8,128)(2,1)S(1)} %get-tuple-element.15.solved, f32[128,128]{1,0:T(8,128)S(1)} %shard_map.87.after), custom_call_target="tpu_custom_call" | custom-call | bytes 65536 | tf_op jit(solution)/shard_map/pallas_call | solution.py:105
  23.8 0.0 collective-permute-done.6.came
  (7 shorter events, 0.1 us)
Async XLA Ops:
  0.6 5.6 %collective-permute-start = (f32[128,128]{1,0:T(8,128)}, f32[128,128]{1,0:T(8,128)S(1)}, u32[]{:S(2)}, u32[]{:S(2)}) collective-permute-start(f32[128,128]{1,0:T(8,128)} %bitcast.10), channel_id=1, source_target_pairs={{0,2},{2,0},{4,6},{6,4},{8,10},{10,8},{12,14},{14,12},{5,3},{3,1},... | collective-permute-start | bytes 196616 | tf_op jit(solution)/shard_map/ppermute | solution.py:193
  6.0 1.4 %collective-permute-start.1 = (f32[256,128]{1,0:T(8,128)S(1)}, f32[256,128]{1,0:T(8,128)S(1)}, u32[]{:S(2)}, u32[]{:S(2)}) collective-permute-start(f32[256,128]{1,0:T(8,128)S(1)} %get-tuple-element.17), channel_id=1, source_target_pairs={{0,1},{1,0},{2,3},{3,2},{4,5},{5,4},{6,7},{7,6},{8,9},{9,8},{10,11... | collective-permute-start | bytes 393224 | tf_op jit(solution)/shard_map/ppermute | solution.py:197
  7.4 1.3 %collective-permute-start.2 = (f32[128,128]{1,0:T(8,128)S(1)}, f32[128,128]{1,0:T(8,128)S(1)}, u32[]{:S(2)}, u32[]{:S(2)}) collective-permute-start(f32[128,128]{1,0:T(8,128)S(1)} %fusion), channel_id=1, source_target_pairs={{0,1},{1,0},{2,3},{3,2},{4,5},{5,4},{6,7},{7,6},{8,9},{9,8},{10,11... | collective-permute-start | bytes 196616 | tf_op jit(solution)/shard_map/ppermute | solution.py:200
  8.9 6.0 %collective-permute-start.3 = (f32[128,256]{1,0:T(8,128)S(1)}, f32[128,256]{1,0:T(8,128)S(1)}, u32[]{:S(2)}, u32[]{:S(2)}) collective-permute-start(f32[128,256]{1,0:T(8,128)S(1)} %pad_maximum_fusion.own), channel_id=1, source_target_pairs={{0,2},{1,5},{2,0},{3,7},{4,6},{5,1},{6,4},{7,3},{8,10},{9,13},{10,... | collective-permute-start | bytes 393224 | tf_op jit(solution)/shard_map/ppermute | solution.py:222
  10.4 6.1 %collective-permute-start.4 = (f32[128,256]{1,0:T(8,128)S(1)}, f32[128,256]{1,0:T(8,128)S(1)}, u32[]{:S(2)}, u32[]{:S(2)}) collective-permute-start(f32[128,256]{1,0:T(8,128)S(1)} %pad_maximum_fusion.own), channel_id=1, source_target_pairs={{0,4},{1,3},{2,6},{3,1},{4,0},{5,7},{6,2},{7,5},{8,12},{9,11},{10,... | collective-permute-start | bytes 393224 | tf_op jit(solution)/shard_map/ppermute | solution.py:222
  11.9 6.2 %collective-permute-start.5 = (f32[128,256]{1,0:T(8,128)S(1)}, f32[128,256]{1,0:T(8,128)S(1)}, u32[]{:S(2)}, u32[]{:S(2)}) collective-permute-start(f32[128,256]{1,0:T(8,128)S(1)} %pad_maximum_fusion.own), channel_id=1, source_target_pairs={{0,6},{1,7},{2,4},{3,5},{4,2},{5,3},{6,0},{7,1},{8,14},{9,15},{10,... | collective-permute-start | bytes 393224 | tf_op jit(solution)/shard_map/ppermute | solution.py:222
  18.6 5.2 %collective-permute-start.6 = (f32[128,128]{1,0:T(8,128)S(1)}, f32[128,128]{1,0:T(8,128)S(1)}, u32[]{:S(2)}, u32[]{:S(2)}) collective-permute-start(f32[128,128]{1,0:T(8,128)S(1)} %shard_map.87.after), channel_id=1, source_target_pairs={{0,8},{2,10},{4,12},{6,14},{8,0},{10,2},{12,4},{14,6},{1,9},{3,11}... | collective-permute-start | bytes 196616 | tf_op jit(solution)/shard_map/ppermute | solution.py:213
